TPU v7x, 128 devices: a whole 4x4x4 slice. The times are simulated.
128 devices in a mesh: seq: 16 (over y, x), exp: 8 (over z, core).
Axes of the slice: x: 4, y: 4, z: 4, core: 2. Of those that a mesh axis runs over, the one named last changes fastest.
Arguments:
- stream: bfloat16 [2048, 4096], P('seq', 'exp'), may hold values from -6 to 6
- mixer_in: bfloat16 [2048, 8192], P('seq', 'exp'), may hold values from -6 to 6
- gate_in: bfloat16 [2048, 8192], P('seq', 'exp'), may hold values from -6 to 6
- dt_raw: bfloat16 [2048, 8192], P('seq', 'exp'), may hold values from -2 to 13
- dt_bias: float32 [8192], P('exp'), may hold values from -13 to -2
- a_log: float32 [8192, 16], P('exp'), may hold values from -1.2 to 0.7
- conv_weight: float32 [8192, 4], P('exp'), may hold values from -3 to 3
- conv_bias: float32 [8192], P('exp'), may hold values from -6 to 6
- b_proj: float32 [2048, 16], P('seq'), may hold values from -6 to 6
- c_proj: float32 [2048, 16], P('seq'), may hold values from -6 to 6
- d_skip: float32 [8192], P('exp'), may hold values from 0.3 to 3
- w_out: bfloat16 [8192, 4096], P('exp', 'seq'), may hold values from -0.0625 to 0.0625
- expert_index: int32 [2048, 2], P('seq'), may hold values from 0 to 7, all different within a row; in each aligned block of 128 rows (0 to 127, 128 to 255, ...) at most 48 rows name the same one
- gate_weights: float32 [2048, 2], P('seq'), may hold values from 0.05 to 0.6
- norm_gain: float32 [4096], replicated, may hold values from 0.1 to 1.9
- w_gate: bfloat16 [8, 4096, 12288], P('exp', None, 'seq'), may hold values from -0.09375 to 0.09375
- w_up: bfloat16 [8, 4096, 12288], P('exp', None, 'seq'), may hold values from -0.09375 to 0.09375
- w_down: bfloat16 [8, 12288, 4096], P('exp', 'seq'), may hold values from -0.0546875 to 0.0546875
Outputs:
- block_out: bfloat16 [2048, 4096], P('seq', 'exp')
Inputs may be any that keep to these rules, and one draw needn't show every extreme that they name: `expert_index`: the two experts of a position differ. Among the 128 positions of one seq shard (aligned blocks), no expert is chosen by more than 48 routes, and in every draw some expert is chosen by exactly 48.
All inputs are finite; a program needn't handle non-finite values.
Results may differ from a plain program's by a relative error of at most 0.012.
Values may be sent and summed in bfloat16 or wider, within the bound.
No kernel may reach another device: no remote copies, remote signals or barrier semaphores. Data moves between devices by JAX's collectives and lax.ppermute only.
A program may use at most 192 MiB of HBM per device.

v0:
```python
import jax
import jax.numpy as jnp
from jax import lax
from jax.experimental import pallas as pl
from jax.experimental.pallas import tpu as pltpu
from jax.sharding import PartitionSpec as P

KCONV = 4
SIDE = 4
STATES = 16
LOG2E = 1.4426950408889634
F32 = jnp.float32
BF16 = jnp.bfloat16


def shift(value, axis, distance):
    cells = [(y, x) for y in range(SIDE) for x in range(SIDE)]
    if axis == "x":
        route = [(y * SIDE + x, y * SIDE + (x + distance) % SIDE) for y, x in cells]
    else:
        route = [(y * SIDE + x, (y + distance) % SIDE * SIDE + x) for y, x in cells]
    return lax.ppermute(value, "seq", route)


def partner(value):
    cells = range(SIDE * SIDE)
    return lax.ppermute(value, "seq", [(i, i ^ 1) for i in cells])


def ring_gather(block, axis):
    return [block] + [shift(block, axis, distance) for distance in range(1, SIDE)]


def relay_gather(blocks, axis):
    half = blocks.shape[0] // 2
    before = shift(blocks, axis, 1)
    after = shift(blocks, axis, -1)
    far = [shift(before[:half], axis, 1), shift(after[half:], axis, -1)]
    return [blocks, before, jnp.concatenate(far), after]


def grid_gather(block, order):
    near = jnp.stack(ring_gather(block, order[0]))
    return relay_gather(near, order[1])


def ring_scatter(blocks, axis):
    total = blocks[0].astype(F32)
    for k in (1, 3, 2):
        total = total + shift(blocks[k].astype(BF16), axis, -k).astype(F32)
    return total


def relay_scatter(blocks, axis):
    own, minus, far, plus = blocks
    half = far.shape[0] // 2
    via_plus = shift(far[:half], axis, 1).astype(F32)
    via_minus = shift(far[half:], axis, -1).astype(F32)
    plus = jnp.concatenate([(plus[:half].astype(F32) + via_plus).astype(BF16), plus[half:]])
    minus = jnp.concatenate([minus[:half], (minus[half:].astype(F32) + via_minus).astype(BF16)])
    total = own.astype(F32) + shift(plus, axis, 1).astype(F32)
    return total + shift(minus, axis, -1).astype(F32)


def fetch(sources, targets, semaphores):
    copies = [
        pltpu.make_async_copy(source, target, semaphores.at[i])
        for i, (source, target) in enumerate(zip(sources, targets))
    ]
    for copy in copies:
        copy.start()
    for copy in copies:
        copy.wait()


def copies_of(arrays):
    return [pltpu.VMEM(array.shape, array.dtype) for array in arrays] + [
        pltpu.SemaphoreType.DMA((len(arrays),))
    ]


def first_pass(x_hbm, dt_hbm, rim_ref, dtb_ref, cw_ref, cb_ref, rate_ref, b_ref,
               step_ref, act_ref, fin_ref, pad_ref, x_ref, dt_ref, semaphores):
    tokens, channels = x_ref.shape
    fetch((x_hbm, dt_hbm), (x_ref, dt_ref), semaphores)
    lanes = 128
    pad_ref[8 : 8 + tokens, :] = x_ref[...].astype(F32)
    pad_ref[0:8, :] = rim_ref[...].astype(F32)

    def columns(k, carry):
        cols = pl.ds(pl.multiple_of(k * lanes, lanes), lanes)
        total = cb_ref[:, cols]
        for tap in range(KCONV):
            low = 8 - (KCONV - 1) + tap
            total = total + cw_ref[tap : tap + 1, cols] * pad_ref[low : low + tokens, cols]
        act_ref[:, k, :] = total * jax.nn.sigmoid(total)
        raw = dt_ref[:, cols].astype(F32) + dtb_ref[:, cols]
        step_ref[:, k, :] = jnp.maximum(raw, 0.0) + jnp.log1p(jnp.exp(-jnp.abs(raw)))
        return carry

    lax.fori_loop(0, channels // lanes, columns, 0)

    def advance(t, carry):
        states, summed = carry
        step = step_ref[t]
        source = step * act_ref[t]
        states = tuple(
            jnp.exp2(step * rate_ref[n]) * states[n] + b_ref[t, n] * source for n in range(STATES)
        )
        return states, summed + step

    zero = jnp.zeros((8, lanes), F32)
    states, summed = lax.fori_loop(0, tokens, advance, ((zero,) * STATES, zero), unroll=2)
    for n in range(STATES):
        fin_ref[n] = states[n]
    fin_ref[STATES] = summed


def second_pass(step_hbm, act_hbm, gate_hbm, enter_ref, rate_ref, skip_ref, b_ref, c_ref,
                out_ref, y_ref, step_ref, act_ref, gate_ref, semaphores):
    tokens, channels = gate_ref.shape
    fetch((step_hbm, act_hbm, gate_hbm), (step_ref, act_ref, gate_ref), semaphores)
    lanes = 128
    skip = skip_ref[...]

    def advance(t, states):
        step = step_ref[t]
        act = act_ref[t]
        source = step * act
        sums = [skip * act, None]
        after = []
        for n in range(STATES):
            state = jnp.exp2(step * rate_ref[n]) * states[n] + b_ref[t, n] * source
            term = c_ref[t, n] * state
            sums[n % 2] = term if sums[n % 2] is None else sums[n % 2] + term
            after.append(state)
        y_ref[t] = sums[0] + sums[1]
        return tuple(after)

    lax.fori_loop(0, tokens, advance, tuple(enter_ref[n] for n in range(STATES)), unroll=2)

    def columns(k, carry):
        cols = pl.ds(pl.multiple_of(k * lanes, lanes), lanes)
        gate = gate_ref[:, cols].astype(F32)
        out_ref[:, cols] = (y_ref[:, k, :] * (gate * jax.nn.sigmoid(gate))).astype(BF16)
        return carry

    lax.fori_loop(0, channels // lanes, columns, 0)


def entering_state(final, rate, ahead, after):
    along_x = lax.axis_index("seq") % SIDE
    along_y = lax.axis_index("seq") // SIDE

    def chain(earlier, latter):
        decay = jnp.exp2(rate * latter[1])
        return decay * earlier[0] + latter[0], earlier[1] + latter[1]

    def masked(pair, reached):
        return jnp.where(reached, pair[0], 0.0), jnp.where(reached, pair[1], 0.0)

    def split(packed):
        return packed[:STATES], packed[STATES]

    def spread(packed, axis, place):
        others = [split(shift(packed, axis, d)) for d in range(1, SIDE)]
        before = masked(others[2], place >= 3)
        for d in (2, 1):
            before = chain(before, masked(others[d - 1], place >= d))
        return before, others

    own = split(final)
    before_x, others = spread(final, "x", along_x)
    total = chain(before_x, own)
    for d in (3, 2, 1):
        total = chain(total, masked(others[d - 1], along_x < d))
    packed = jnp.concatenate([total[0], total[1][None]], 0)
    packed, after = lax.optimization_barrier((packed, after))
    far = shift(after, "x", 2)
    packed, ahead = lax.optimization_barrier((packed, ahead))
    before_y, _ = spread(packed, "y", along_y)
    return chain(before_y, before_x)[0], ahead, [after, far]


def mixer(
    mixer_in, gate_in, dt_raw, dt_bias, a_log, conv_weight, conv_bias, b_proj, c_proj, d_skip, w_out
):
    tokens, channels = mixer_in.shape
    count, index = lax.axis_size("seq"), lax.axis_index("seq")
    rim = lax.ppermute(mixer_in[tokens - 8 :], "seq", [(i, i + 1) for i in range(count - 1)])
    split = 7 * channels // 16
    low, high = w_out[:split], w_out[split:]
    low_pair = jnp.stack([low, shift(low, "x", 2)])
    dt_raw, low_pair = lax.optimization_barrier((dt_raw, low_pair))
    high_ring = ring_gather(high, "y")
    rate = (-LOG2E * jnp.exp(a_log)).T.reshape(STATES, 8, 128)
    smem = pl.BlockSpec(memory_space=pltpu.SMEM)
    wide = jax.ShapeDtypeStruct((tokens, 8, 128), F32)
    ends = jax.ShapeDtypeStruct((STATES + 1, 8, 128), F32)
    vmem = pl.BlockSpec(memory_space=pltpu.VMEM)
    stay = pl.BlockSpec(memory_space=pltpu.HBM)
    step, act, final = pl.pallas_call(
        first_pass,
        out_shape=(wide, wide, ends),
        in_specs=[stay] * 2 + [vmem] * 5 + [smem],
        out_specs=[vmem] * 3,
        scratch_shapes=[pltpu.VMEM((tokens + 8, channels), F32), *copies_of((mixer_in, dt_raw))],
        compiler_params=pltpu.CompilerParams(vmem_limit_bytes=58 << 20),
        name="scan_state",
    )(mixer_in, dt_raw, rim, dt_bias[None, :], conv_weight.T, conv_bias[None, :], rate, b_proj)
    final, high_ring = lax.optimization_barrier((final, high_ring))
    first = ring_gather(low_pair, "y")
    high_ring = jnp.stack(high_ring)
    enter, first, second = entering_state(final, rate, first, high_ring)
    mixed = pl.pallas_call(
        second_pass,
        out_shape=jax.ShapeDtypeStruct((tokens, channels), BF16),
        in_specs=[stay] * 3 + [vmem] * 3 + [smem] * 2,
        out_specs=vmem,
        scratch_shapes=[pltpu.VMEM((tokens, 8, 128), F32), *copies_of((step, act, gate_in))],
        compiler_params=pltpu.CompilerParams(vmem_limit_bytes=58 << 20),
        name="scan_output",
    )(step, act, gate_in, enter, rate, d_skip.reshape(8, 128), b_proj, c_proj)
    return mixed, (first, second)


def project_kernel(place_ref, own_ref, other_ref, *refs):
    count = SIDE + 2
    out_ref, rows, first, second, semaphores = refs[count:]
    targets = [first.at[i] for i in range(SIDE)] + [second.at[j] for j in range(2)]
    fetch(refs[:count], targets, semaphores)
    tokens = own_ref.shape[0]
    rows[:tokens] = own_ref[...]
    rows[tokens:] = other_ref[...]
    split = first.shape[2]
    y, side = place_ref[0], place_ref[1]

    def one(step, carry):
        i, j = step // 2, step % 2
        owner = lax.rem(y - i + SIDE, SIDE) * 2 + lax.rem(side + j, 2)
        total = jnp.dot(rows[:, :split], first[i, j], preferred_element_type=F32)
        total += jnp.dot(rows[:, split:], second[j, i], preferred_element_type=F32)
        total = total.astype(BF16)
        out_ref[owner, 0] = total[:tokens]
        out_ref[owner, 1] = total[tokens:]
        return carry

    lax.fori_loop(0, 2 * SIDE, one, 0)


def project(mixed, weights):
    first, second = weights
    tokens, columns = mixed.shape[0], first[0].shape[2]
    index = lax.axis_index("seq")
    place = jnp.stack([index // SIDE, index % SIDE // 2]).astype(jnp.int32)
    vmem = pl.BlockSpec(memory_space=pltpu.VMEM)
    stay = pl.BlockSpec(memory_space=pltpu.HBM)
    partial = pl.pallas_call(
        project_kernel,
        out_shape=jax.ShapeDtypeStruct((2 * SIDE, 2, tokens, columns), BF16),
        in_specs=[pl.BlockSpec(memory_space=pltpu.SMEM)] + [vmem] * 2 + [stay] * (SIDE + 2),
        out_specs=vmem,
        scratch_shapes=[
            pltpu.VMEM((2 * tokens, mixed.shape[1]), BF16),
            pltpu.VMEM((SIDE, *first[0].shape), BF16),
            pltpu.VMEM((2, *second[0].shape), BF16),
            pltpu.SemaphoreType.DMA((SIDE + 2,)),
        ],
        compiler_params=pltpu.CompilerParams(vmem_limit_bytes=58 << 20),
        name="project",
    )(place, mixed, partner(mixed), *first, *second)
    partial = lax.all_to_all(partial, "exp", split_axis=0, concat_axis=0)
    total = jnp.sum(partial.astype(F32), axis=0)
    other = partner(total[1].astype(BF16)).astype(F32)
    is_even = lax.axis_index("seq") % 2 == 0
    return jnp.concatenate(
        [jnp.where(is_even, total[0], other), jnp.where(is_even, other, total[0])], axis=1
    )


def local(
    stream,
    mixer_in,
    gate_in,
    dt_raw,
    dt_bias,
    a_log,
    conv_weight,
    conv_bias,
    b_proj,
    c_proj,
    d_skip,
    w_out,
    expert_index,
    gate_weights,
    norm_gain,
    w_gate,
    w_up,
    w_down,
):
    tokens = mixer_in.shape[0]
    experts = lax.axis_size("exp")
    groups = lax.axis_size("seq")
    capacity = 3 * tokens // experts
    width = stream.shape[1]
    mixed, weights = mixer(
        mixer_in, gate_in, dt_raw, dt_bias, a_log, conv_weight, conv_bias, b_proj, c_proj, d_skip, w_out
    )
    projected = project(mixed, weights)
    middle = (stream.astype(F32) + projected).astype(BF16)

    flat_exp = expert_index.reshape(-1)
    onehot = (flat_exp[:, None] == jnp.arange(experts, dtype=jnp.int32)[None, :]).astype(jnp.int32)
    ranks = jnp.cumsum(onehot, axis=0) - onehot
    slots = jnp.sum(ranks * onehot, axis=1)
    slot_id = (flat_exp * capacity + slots).reshape(tokens, 2)
    places = jnp.arange(experts * capacity, dtype=jnp.int32)
    chosen = (
        (slot_id[:, 0][None, :] == places[:, None]) | (slot_id[:, 1][None, :] == places[:, None])
    ).astype(BF16)
    outgoing = jnp.dot(chosen, middle, preferred_element_type=F32).astype(BF16)
    outgoing = outgoing.reshape(experts, capacity, width)
    arrived = lax.all_to_all(outgoing, "exp", split_axis=0, concat_axis=2, tiled=True)[0].astype(F32)
    mean_square = jnp.mean(arrived * arrived, axis=1, keepdims=True)
    normed = (arrived * lax.rsqrt(mean_square + 1e-05) * norm_gain[None, :]).astype(BF16)

    half = capacity // 2
    first = grid_gather(normed[:half], "xy")
    second = grid_gather(normed[half:], "yx")

    def feed(offsets):
        rows = jnp.stack([part[k] for part in (first, second) for k in offsets])
        flat = rows.reshape(-1, rows.shape[-1])
        gate_proj = jnp.dot(flat, w_gate[0], preferred_element_type=F32)
        up_proj = jnp.dot(flat, w_up[0], preferred_element_type=F32)
        hidden = lax.optimization_barrier((jax.nn.silu(gate_proj) * up_proj).astype(BF16))
        out = jnp.dot(hidden, w_down[0], preferred_element_type=F32).astype(BF16)
        return out.reshape((2, len(offsets)) + rows.shape[1:])

    fed = {}
    for offsets in ((0,), (1, 3), (2,)):
        out = feed(offsets)
        for at, k in enumerate(offsets):
            fed[k] = out[:, at]
    sums = []
    for which, order in ((0, "yx"), (1, "xy")):
        near = relay_scatter([fed[k][which] for k in range(SIDE)], order[0])
        sums.append(ring_scatter([near[k] for k in range(SIDE)], order[1]))
    summed = jnp.concatenate(sums, 0).astype(BF16)
    summed = summed.reshape(capacity, experts, width).transpose(1, 0, 2)
    returned = lax.all_to_all(summed, "exp", split_axis=0, concat_axis=0)
    returned = returned.reshape(experts * capacity, width)
    expert_sum = 0.0
    for k in range(2):
        pick = (slot_id[:, k][:, None] == places[None, :]).astype(BF16)
        picked = jnp.dot(pick, returned, preferred_element_type=F32)
        expert_sum = expert_sum + gate_weights[:, k][:, None] * picked
    return (middle.astype(F32) + expert_sum).astype(BF16)


def solution(mesh):
    return jax.shard_map(
        local,
        mesh=mesh,
        in_specs=(
            P("seq", "exp"),
            P("seq", "exp"),
            P("seq", "exp"),
            P("seq", "exp"),
            P("exp"),
            P("exp", None),
            P("exp", None),
            P("exp"),
            P("seq", None),
            P("seq", None),
            P("exp"),
            P("exp", "seq"),
            P("seq", None),
            P("seq", None),
            P(),
            P("exp", None, "seq"),
            P("exp", None, "seq"),
            P("exp", "seq", None),
        ),
        out_specs=P("seq", "exp"),
        check_vma=False,
    )
```

profile of v0, /device:TPU:1, one launch (start us, length us, event | category | flops | bytes accessed | tf_op | source)
XLA Modules:
  0.0 237.8 jit_solution(7500854614220682226)
XLA Ops:
  1.0 3.7 %collective-permute-start = (bf16[448,256]{1,0:T(8,128)(2,1)S(1)}, bf16[448,256]{1,0:T(8,128)(2,1)S(1)}, u32[]{:S(2)}, u32[]{:S(2)}) collective-permute-start(bf16[448,256]{1,0:T(8,128)(2,1)S(1)} %get-tuple-element.70), channel_id=1, source_target_pairs={{0,16},{8,24},{16,0},{24,8},{32,48},{40,56},{48,32},{56,40},{64,80... | collective-permute-start | bytes 688136 | tf_op jit(solution)/shard_map/ppermute | solution.py:22
  5.6 2.8 %collective-permute-start.4 = (bf16[576,256]{1,0:T(8,128)(2,1)S(1)}, bf16[576,256]{1,0:T(8,128)(2,1)S(1)}, u32[]{:S(2)}, u32[]{:S(2)}) collective-permute-start(bf16[576,256]{1,0:T(8,128)(2,1)S(1)} %slice.228), channel_id=1, source_target_pairs={{0,96},{8,104},{16,112},{24,120},{32,0},{40,8},{48,16},{56,24},{64... | collective-permute-start | bytes 884744 | tf_op jit(solution)/shard_map/ppermute | solution.py:22
  10.2 2.2 collective-permute-start.1
  12.4 1.4 copy.48.b_ref
  15.4 2.1 collective-permute-start.10
  18.9 7.3 %scan_state.1 = (f32[128,8,128]{2,1,0:T(8,128)}, f32[128,8,128]{2,1,0:T(8,128)}, f32[17,8,128]{2,1,0:T(8,128)}) custom-call(bf16[128,1024]{1,0:T(8,128)(2,1)} %x_hbm.1, bf16[128,1024]{1,0:T(8,128)(2,1)} %dt_hbm, bf16[8,1024]{1,0:T(8,128)(2,1)} %copy-done.10, f32[1,1024]{1,0:T(1,128)} %bitcast.267, f32[4,1024]{1,0:T(4,128)} %bitcast.266, ...), custom_call_target="tpu_custom_call" | custom-call | tf_op jit(solution)/shard_map/scan_state/pallas_call | solution.py:202
  27.1 2.5 %collective-permute-start.6 = (f32[17,8,128]{2,1,0:T(8,128)}, f32[17,8,128]{2,1,0:T(8,128)S(1)}, u32[]{:S(2)}, u32[]{:S(2)}) collective-permute-start(f32[17,8,128]{2,1,0:T(8,128)} %get-tuple-element.26), channel_id=1, source_target_pairs={{0,16},{8,24},{16,0},{24,8},{32,48},{40,56},{48,32},{56,40},{64,80... | collective-permute-start | bytes 208904 | tf_op jit(solution)/shard_map/ppermute | solution.py:22
  35.3 2.0 collective-permute-start.15
  37.3 4.1 %collective-permute-done.8.refs_1_ = bf16[2,448,256]{2,1,0:T(8,128)(2,1)S(1)} collective-permute-done((bf16[2,448,256]{2,1,0:T(8,128)(2,1)S(1)}, bf16[2,448,256]{2,1,0:T(8,128)(2,1)S(1)}, u32[]{:S(2)}, u32[]{:S(2)}) %collective-permute-start.8) | collective-permute-done | bytes 458784 | tf_op jit(solution)/shard_map/ppermute | solution.py:22
  42.8 1.4 copy.50.c_ref
  44.2 2.0 collective-permute-start.13
  48.1 3.0 %collective-permute-done.11 = f32[17,8,128]{2,1,0:T(8,128)S(1)} collective-permute-done((f32[17,8,128]{2,1,0:T(8,128)}, f32[17,8,128]{2,1,0:T(8,128)S(1)}, u32[]{:S(2)}, u32[]{:S(2)}) %collective-permute-start.11) | collective-permute-done | bytes 69664 | tf_op jit(solution)/shard_map/ppermute | solution.py:22
  51.1 1.6 fusion.67.enter_ref
  52.6 8.5 %scan_output.1.own_ref = bf16[128,1024]{1,0:T(8,128)(2,1)} custom-call(f32[128,8,128]{2,1,0:T(8,128)} %get-tuple-element.23.step_hbm, f32[128,8,128]{2,1,0:T(8,128)} %get-tuple-element.24.act_hbm, bf16[128,1024]{1,0:T(8,128)(2,1)} %gate_hbm.1, f32[16,8,128]{2,1,0:T(8,128)} %fusion.67.enter_ref, f32[16,8,128]{2,1,0:T(8,128)} %bitcast.240, ...), custom_call_target="tpu_custom_call" | custom-call | tf_op jit(solution)/shard_map/scan_output/pallas_call | solution.py:215
  62.2 4.5 %collective-permute-done.14.other_ref = bf16[128,1024]{1,0:T(8,128)(2,1)} collective-permute-done((bf16[128,1024]{1,0:T(8,128)(2,1)}, bf16[128,1024]{1,0:T(8,128)(2,1)}, u32[]{:S(2)}, u32[]{:S(2)}) %collective-permute-start.14) | collective-permute-done | bytes 262176 | tf_op jit(solution)/shard_map/ppermute | solution.py:27
  67.8 7.4 %project.1 = bf16[8,2,128,256]{3,2,1,0:T(8,128)(2,1)} custom-call(s32[2]{0:T(128)} %pad_add_fusion.place_ref, bf16[128,1024]{1,0:T(8,128)(2,1)} %scan_output.1.own_ref, bf16[128,1024]{1,0:T(8,128)(2,1)} %collective-permute-done.14.other_ref, bf16[2,448,256]{2,1,0:T(8,128)(2,1)} %copy-done.1, bf16[2,448,256]{2,1,0:T(8,128)(2,1)} %copy-done.7, ...), custom_call_target="tpu_custom_call" | custom-call | tf_op jit(solution)/shard_map/project/pallas_call | solution.py:258
  75.2 10.8 %all-to-all-start = ((bf16[8,2,128,256]{3,2,1,0:T(8,128)(2,1)}), bf16[8,2,128,256]{3,2,1,0:T(8,128)(2,1)S(1)}, u32[]{:S(2)}, u32[]{:S(2)}) async-start(bf16[8,2,128,256]{3,2,1,0:T(8,128)(2,1)} %project.1), calls=%async_computation | async-start | bytes 2097152 | tf_op jit(solution)/shard_map/all_to_all | solution.py:272
  87.6 13.5 %all-to-all-done = bf16[8,2,128,256]{3,2,1,0:T(8,128)(2,1)S(1)} async-done(((bf16[8,2,128,256]{3,2,1,0:T(8,128)(2,1)}), bf16[8,2,128,256]{3,2,1,0:T(8,128)(2,1)S(1)}, u32[]{:S(2)}, u32[]{:S(2)}) %all-to-all-start) | async-done | bytes 1048608 | tf_op jit(solution)/shard_map/all_to_all | solution.py:272
  101.7 2.8 %collective-permute-done.16 = bf16[128,256]{1,0:T(8,128)(2,1)S(1)} collective-permute-done((bf16[128,256]{1,0:T(8,128)(2,1)S(1)}, bf16[128,256]{1,0:T(8,128)(2,1)S(1)}, u32[]{:S(2)}, u32[]{:S(2)}) %collective-permute-start.16) | collective-permute-done | bytes 65568 | tf_op jit(solution)/shard_map/ppermute | solution.py:27
  104.8 12.5 %all_to_all.19 = bf16[8,48,512]{2,1,0:T(8,128)(2,1)S(1)} all-to-all(bf16[8,48,512]{2,1,0:T(8,128)(2,1)S(1)} %bitcast.245), channel_id=1, replica_groups=mesh['seq'=16,'exp'=8] {'exp'}, dimensions={0} | all-to-all | bytes 786432 | tf_op jit(solution)/shard_map/all_to_all | solution.py:323
  119.7 1.6 collective-permute-start.22
  122.8 2.6 %collective-permute-done.21 = bf16[24,4096]{1,0:T(8,128)(2,1)S(1)} collective-permute-done((bf16[24,4096]{1,0:T(8,128)(2,1)S(1)}, bf16[24,4096]{1,0:T(8,128)(2,1)S(1)}, u32[]{:S(2)}, u32[]{:S(2)}) %collective-permute-start.21) | collective-permute-done | bytes 196640 | tf_op jit(solution)/shard_map/ppermute | solution.py:22
  126.5 4.3 %collective-permute-done.20 = bf16[24,4096]{1,0:T(8,128)(2,1)S(1)} collective-permute-done((bf16[24,4096]{1,0:T(8,128)(2,1)S(1)}, bf16[24,4096]{1,0:T(8,128)(2,1)S(1)}, u32[]{:S(2)}, u32[]{:S(2)}) %collective-permute-start.20) | collective-permute-done | bytes 196640 | tf_op jit(solution)/shard_map/ppermute | solution.py:22
  131.2 2.6 %collective-permute-start.26 = (bf16[4,24,4096]{2,1,0:T(8,128)(2,1)S(1)}, bf16[4,24,4096]{2,1,0:T(8,128)(2,1)S(1)}, u32[]{:S(2)}, u32[]{:S(2)}) collective-permute-start(bf16[4,24,4096]{2,1,0:T(8,128)(2,1)S(1)} %get-tuple-element.68), channel_id=1, source_target_pairs={{0,24},{8,0},{16,8},{24,16},{32,56},{40,32},{48,40},{56,48},{64,88... | collective-permute-start | bytes 2359304 | tf_op jit(solution)/shard_map/ppermute | solution.py:22
  134.2 2.7 %collective-permute-start.24 = (bf16[4,24,4096]{2,1,0:T(8,128)(2,1)S(1)}, bf16[4,24,4096]{2,1,0:T(8,128)(2,1)S(1)}, u32[]{:S(2)}, u32[]{:S(2)}) collective-permute-start(bf16[4,24,4096]{2,1,0:T(8,128)(2,1)S(1)} %get-tuple-element.66), channel_id=1, source_target_pairs={{0,96},{8,104},{16,112},{24,120},{32,0},{40,8},{48,16},{56,24},{64... | collective-permute-start | bytes 2359304 | tf_op jit(solution)/shard_map/ppermute | solution.py:22
  137.1 1.4 fusion.16
  139.8 1.4 fusion.38
  143.3 7.7 %collective-permute-done.25 = bf16[4,24,4096]{2,1,0:T(8,128)(2,1)S(1)} collective-permute-done((bf16[4,24,4096]{2,1,0:T(8,128)(2,1)S(1)}, bf16[4,24,4096]{2,1,0:T(8,128)(2,1)S(1)}, u32[]{:S(2)}, u32[]{:S(2)}) %collective-permute-start.25) | collective-permute-done | bytes 786464 | tf_op jit(solution)/shard_map/ppermute | solution.py:22
  151.1 2.7 %collective-permute-start.30 = (bf16[2,24,4096]{2,1,0:T(8,128)(2,1)S(1)}, bf16[2,24,4096]{2,1,0:T(8,128)(2,1)S(1)}, u32[]{:S(2)}, u32[]{:S(2)}) collective-permute-start(bf16[2,24,4096]{2,1,0:T(8,128)(2,1)S(1)} %slice.307), channel_id=1, source_target_pairs={{0,24},{8,0},{16,8},{24,16},{32,56},{40,32},{48,40},{56,48},{64,88... | collective-permute-start | bytes 1179656 | tf_op jit(solution)/shard_map/ppermute | solution.py:22
  154.0 2.7 %collective-permute-start.28 = (bf16[2,24,4096]{2,1,0:T(8,128)(2,1)S(1)}, bf16[2,24,4096]{2,1,0:T(8,128)(2,1)S(1)}, u32[]{:S(2)}, u32[]{:S(2)}) collective-permute-start(bf16[2,24,4096]{2,1,0:T(8,128)(2,1)S(1)} %slice.305), channel_id=1, source_target_pairs={{0,96},{8,104},{16,112},{24,120},{32,0},{40,8},{48,16},{56,24},{64... | collective-permute-start | bytes 1179656 | tf_op jit(solution)/shard_map/ppermute | solution.py:22
  157.1 2.6 %fusion.14 = f32[384,768]{1,0:T(8,128)S(1)} fusion(bf16[384,4096]{1,0:T(8,128)(2,1)S(1)} %bitcast.228, bf16[1,4096,768]{2,1,0:T(8,128)(2,1)S(1)} %bitcast.271), kind=kOutput, calls=%fused_computation.14 | convolution fusion | flops 2415919104 | bytes 10616832 | tf_op jit(solution)/shard_map/dot_general | solution.py:334
  159.7 2.7 %multiply_convert_fusion = bf16[384,768]{1,0:T(8,128)(2,1)S(1)} fusion(f32[384,768]{1,0:T(8,128)S(1)} %fusion.14, bf16[384,4096]{1,0:T(8,128)(2,1)S(1)} %bitcast.229, bf16[1,4096,768]{2,1,0:T(8,128)(2,1)S(1)} %bitcast.273), kind=kOutput, calls=%fused_computation.35 | convolution fusion | flops 2417688576 | bytes 11206656 | tf_op jit(solution)/shard_map/dot_general | solution.py:335
  162.4 2.8 %fusion.18 = bf16[384,4096]{1,0:T(8,128)(2,1)S(1)} fusion(bf16[384,768]{1,0:T(8,128)(2,1)S(1)} %multiply_convert_fusion, bf16[1,768,4096]{2,1,0:T(8,128)(2,1)S(1)} %bitcast.275), kind=kOutput, calls=%fused_computation.18 | convolution fusion | flops 2417491968 | bytes 10027008 | tf_op jit(solution)/shard_map/dot_general | solution.py:337
  165.6 1.4 fusion.12
  167.0 1.4 fusion.35
  171.5 2.7 %collective-permute-start.33 = (bf16[2,24,4096]{2,1,0:T(8,128)(2,1)S(1)}, bf16[2,24,4096]{2,1,0:T(8,128)(2,1)S(1)}, u32[]{:S(2)}, u32[]{:S(2)}) collective-permute-start(bf16[2,24,4096]{2,1,0:T(8,128)(2,1)S(1)} %bitcast.251), channel_id=1, source_target_pairs={{0,96},{8,104},{16,112},{24,120},{32,0},{40,8},{48,16},{56,24},{64... | collective-permute-start | bytes 1179656 | tf_op jit(solution)/shard_map/ppermute | solution.py:22
  174.3 3.9 %collective-permute-done.40 = bf16[2,24,4096]{2,1,0:T(8,128)(2,1)S(1)} collective-permute-done((bf16[2,24,4096]{2,1,0:T(8,128)(2,1)S(1)}, bf16[2,24,4096]{2,1,0:T(8,128)(2,1)S(1)}, u32[]{:S(2)}, u32[]{:S(2)}) %collective-permute-start.40) | collective-permute-done | bytes 393248 | tf_op jit(solution)/shard_map/ppermute | solution.py:22
  181.4 1.9 collective-permute-start.41
  183.4 3.2 %collective-permute-start.34 = (bf16[4,24,4096]{2,1,0:T(8,128)(2,1)S(1)}, bf16[4,24,4096]{2,1,0:T(8,128)(2,1)S(1)}, u32[]{:S(2)}, u32[]{:S(2)}) collective-permute-start(bf16[4,24,4096]{2,1,0:T(8,128)(2,1)S(1)} %pad_maximum_fusion.7), channel_id=1, source_target_pairs={{0,96},{8,104},{16,112},{24,120},{32,0},{40,8},{48,16},{56,24},{64... | collective-permute-start | bytes 2359304 | tf_op jit(solution)/shard_map/ppermute | solution.py:22
  186.8 9.8 %collective-permute-done.39 = bf16[4,24,4096]{2,1,0:T(8,128)(2,1)S(1)} collective-permute-done((bf16[4,24,4096]{2,1,0:T(8,128)(2,1)S(1)}, bf16[4,24,4096]{2,1,0:T(8,128)(2,1)S(1)}, u32[]{:S(2)}, u32[]{:S(2)}) %collective-permute-start.39) | collective-permute-done | bytes 786464 | tf_op jit(solution)/shard_map/ppermute | solution.py:22
  197.1 2.8 %collective-permute-start.42 = (bf16[24,4096]{1,0:T(8,128)(2,1)S(1)}, bf16[24,4096]{1,0:T(8,128)(2,1)S(1)}, u32[]{:S(2)}, u32[]{:S(2)}) collective-permute-start(bf16[24,4096]{1,0:T(8,128)(2,1)S(1)} %get-tuple-element.62), channel_id=1, source_target_pairs={{0,96},{8,104},{16,112},{24,120},{32,0},{40,8},{48,16},{56,24},{64... | collective-permute-start | bytes 589832 | tf_op jit(solution)/shard_map/ppermute | solution.py:22
  202.3 1.4 collective-permute-start.35
  203.7 1.9 collective-permute-done.42
  206.2 1.8 collective-permute-done.44
  208.0 2.3 collective-permute-done.43
  210.5 1.6 collective-permute-done.36
  213.3 15.2 %all-to-all-start.2 = ((bf16[8,48,512]{2,1,0:T(8,128)(2,1)}), bf16[8,48,512]{2,1,0:T(8,128)(2,1)S(1)}, u32[]{:S(2)}, u32[]{:S(2)}) async-start(bf16[8,48,512]{2,1,0:T(8,128)(2,1)} %copy.55), calls=%async_computation.2 | async-start | bytes 786432 | tf_op jit(solution)/shard_map/all_to_all | solution.py:351
  228.5 8.1 %all-to-all-done.2 = bf16[8,48,512]{2,1,0:T(8,128)(2,1)S(1)} async-done(((bf16[8,48,512]{2,1,0:T(8,128)(2,1)}), bf16[8,48,512]{2,1,0:T(8,128)(2,1)S(1)}, u32[]{:S(2)}, u32[]{:S(2)}) %all-to-all-start.2) | async-done | bytes 393248 | tf_op jit(solution)/shard_map/all_to_all | solution.py:351
  (171 shorter events, 43.4 us)
Async XLA Ops:
  1.0 14.4 %collective-permute-start = (bf16[448,256]{1,0:T(8,128)(2,1)S(1)}, bf16[448,256]{1,0:T(8,128)(2,1)S(1)}, u32[]{:S(2)}, u32[]{:S(2)}) collective-permute-start(bf16[448,256]{1,0:T(8,128)(2,1)S(1)} %get-tuple-element.70), channel_id=1, source_target_pairs={{0,16},{8,24},{16,0},{24,8},{32,48},{40,56},{48,32},{56,40},{64,80... | collective-permute-start | bytes 688136 | tf_op jit(solution)/shard_map/ppermute | solution.py:22
  5.6 20.6 %collective-permute-start.4 = (bf16[576,256]{1,0:T(8,128)(2,1)S(1)}, bf16[576,256]{1,0:T(8,128)(2,1)S(1)}, u32[]{:S(2)}, u32[]{:S(2)}) collective-permute-start(bf16[576,256]{1,0:T(8,128)(2,1)S(1)} %slice.228), channel_id=1, source_target_pairs={{0,96},{8,104},{16,112},{24,120},{32,0},{40,8},{48,16},{56,24},{64... | collective-permute-start | bytes 884744 | tf_op jit(solution)/shard_map/ppermute | solution.py:22
  8.4 17.8 %collective-permute-start.3 = (bf16[576,256]{1,0:T(8,128)(2,1)S(1)}, bf16[576,256]{1,0:T(8,128)(2,1)S(1)}, u32[]{:S(2)}, u32[]{:S(2)}) collective-permute-start(bf16[576,256]{1,0:T(8,128)(2,1)S(1)} %slice.228), channel_id=1, source_target_pairs={{0,64},{8,72},{16,80},{24,88},{32,96},{40,104},{48,112},{56,120},{... | collective-permute-start | bytes 884744 | tf_op jit(solution)/shard_map/ppermute | solution.py:22
  8.8 17.7 %collective-permute-start.2 = (bf16[576,256]{1,0:T(8,128)(2,1)S(1)}, bf16[576,256]{1,0:T(8,128)(2,1)S(1)}, u32[]{:S(2)}, u32[]{:S(2)}) collective-permute-start(bf16[576,256]{1,0:T(8,128)(2,1)S(1)} %slice.228), channel_id=1, source_target_pairs={{0,32},{8,40},{16,48},{24,56},{32,64},{40,72},{48,80},{56,88},{64,... | collective-permute-start | bytes 884744 | tf_op jit(solution)/shard_map/ppermute | solution.py:22
  10.2 7.3 %collective-permute-start.1 = (bf16[8,1024]{1,0:T(8,128)(2,1)S(1)}, bf16[8,1024]{1,0:T(8,128)(2,1)S(1)}, u32[]{:S(2)}, u32[]{:S(2)}) collective-permute-start(bf16[8,1024]{1,0:T(8,128)(2,1)S(1)} %slice.227), channel_id=1, source_target_pairs={{0,8},{8,16},{16,24},{24,32},{32,40},{40,48},{48,56},{56,64},{64,7... | collective-permute-start | bytes 49160 | tf_op jit(solution)/shard_map/ppermute | solution.py:190
  15.4 21.9 %collective-permute-start.10 = (bf16[2,448,256]{2,1,0:T(8,128)(2,1)S(1)}, bf16[2,448,256]{2,1,0:T(8,128)(2,1)S(1)}, u32[]{:S(2)}, u32[]{:S(2)}) collective-permute-start(bf16[2,448,256]{2,1,0:T(8,128)(2,1)S(1)} %pad_maximum_fusion.10.refs_0_), channel_id=1, source_target_pairs={{0,96},{8,104},{16,112},{24,120},{32,0},{40,8},{48,16},{56,24},{64... | collective-permute-start | bytes 1376264 | tf_op jit(solution)/shard_map/ppermute | solution.py:22
  17.5 19.9 %collective-permute-start.9 = (bf16[2,448,256]{2,1,0:T(8,128)(2,1)S(1)}, bf16[2,448,256]{2,1,0:T(8,128)(2,1)S(1)}, u32[]{:S(2)}, u32[]{:S(2)}) collective-permute-start(bf16[2,448,256]{2,1,0:T(8,128)(2,1)S(1)} %pad_maximum_fusion.10.refs_0_), channel_id=1, source_target_pairs={{0,64},{8,72},{16,80},{24,88},{32,96},{40,104},{48,112},{56,120},{... | collective-permute-start | bytes 1376264 | tf_op jit(solution)/shard_map/ppermute | solution.py:22
  26.4 4.9 %collective-permute-start.7 = (f32[17,8,128]{2,1,0:T(8,128)}, f32[17,8,128]{2,1,0:T(8,128)S(1)}, u32[]{:S(2)}, u32[]{:S(2)}) collective-permute-start(f32[17,8,128]{2,1,0:T(8,128)} %get-tuple-element.26), channel_id=1, source_target_pairs={{0,8},{8,16},{16,24},{24,0},{32,40},{40,48},{48,56},{56,32},{64,72... | collective-permute-start | bytes 208904 | tf_op jit(solution)/shard_map/ppermute | solution.py:22
  27.1 5.5 %collective-permute-start.6 = (f32[17,8,128]{2,1,0:T(8,128)}, f32[17,8,128]{2,1,0:T(8,128)S(1)}, u32[]{:S(2)}, u32[]{:S(2)}) collective-permute-start(f32[17,8,128]{2,1,0:T(8,128)} %get-tuple-element.26), channel_id=1, source_target_pairs={{0,16},{8,24},{16,0},{24,8},{32,48},{40,56},{48,32},{56,40},{64,80... | collective-permute-start | bytes 208904 | tf_op jit(solution)/shard_map/ppermute | solution.py:22
  29.6 3.7 %collective-permute-start.5 = (f32[17,8,128]{2,1,0:T(8,128)}, f32[17,8,128]{2,1,0:T(8,128)S(1)}, u32[]{:S(2)}, u32[]{:S(2)}) collective-permute-start(f32[17,8,128]{2,1,0:T(8,128)} %get-tuple-element.26), channel_id=1, source_target_pairs={{0,24},{8,0},{16,8},{24,16},{32,56},{40,32},{48,40},{56,48},{64,88... | collective-permute-start | bytes 208904 | tf_op jit(solution)/shard_map/ppermute | solution.py:22
  30.3 31.3 %copy-start = (bf16[4,576,256]{2,1,0:T(8,128)(2,1)}, bf16[4,576,256]{2,1,0:T(8,128)(2,1)S(1)}, u32[]{:S(2)}) copy-start(bf16[4,576,256]{2,1,0:T(8,128)(2,1)S(1)} %pad_maximum_fusion.3.refs_4_) | copy-start | bytes 3538948
  31.3 10.2 %collective-permute-start.8 = (bf16[2,448,256]{2,1,0:T(8,128)(2,1)S(1)}, bf16[2,448,256]{2,1,0:T(8,128)(2,1)S(1)}, u32[]{:S(2)}, u32[]{:S(2)}) collective-permute-start(bf16[2,448,256]{2,1,0:T(8,128)(2,1)S(1)} %pad_maximum_fusion.10.refs_0_), channel_id=1, source_target_pairs={{0,32},{8,40},{16,48},{24,56},{32,64},{40,72},{48,80},{56,88},{64,... | collective-permute-start | bytes 1376264 | tf_op jit(solution)/shard_map/ppermute | solution.py:22
  35.3 31.5 %collective-permute-start.15 = (bf16[4,576,256]{2,1,0:T(8,128)(2,1)S(1)}, bf16[4,576,256]{2,1,0:T(8,128)(2,1)S(1)}, u32[]{:S(2)}, u32[]{:S(2)}) collective-permute-start(bf16[4,576,256]{2,1,0:T(8,128)(2,1)S(1)} %pad_maximum_fusion.3.refs_4_), channel_id=1, source_target_pairs={{0,16},{8,24},{16,0},{24,8},{32,48},{40,56},{48,32},{56,40},{64,80... | collective-permute-start | bytes 3538952 | tf_op jit(solution)/shard_map/ppermute | solution.py:22
  42.2 5.2 %collective-permute-start.12 = (f32[17,8,128]{2,1,0:T(8,128)}, f32[17,8,128]{2,1,0:T(8,128)}, u32[]{:S(2)}, u32[]{:S(2)}) collective-permute-start(f32[17,8,128]{2,1,0:T(8,128)} %pad_maximum_fusion.11), channel_id=1, source_target_pairs={{0,64},{8,72},{16,80},{24,88},{32,96},{40,104},{48,112},{56,120},{... | collective-permute-start | bytes 208904 | tf_op jit(solution)/shard_map/ppermute | solution.py:22
  44.2 6.9 %collective-permute-start.13 = (f32[17,8,128]{2,1,0:T(8,128)}, f32[17,8,128]{2,1,0:T(8,128)S(1)}, u32[]{:S(2)}, u32[]{:S(2)}) collective-permute-start(f32[17,8,128]{2,1,0:T(8,128)} %pad_maximum_fusion.11), channel_id=1, source_target_pairs={{0,96},{8,104},{16,112},{24,120},{32,0},{40,8},{48,16},{56,24},{64... | collective-permute-start | bytes 208904 | tf_op jit(solution)/shard_map/ppermute | solution.py:22
  46.2 4.9 %collective-permute-start.11 = (f32[17,8,128]{2,1,0:T(8,128)}, f32[17,8,128]{2,1,0:T(8,128)S(1)}, u32[]{:S(2)}, u32[]{:S(2)}) collective-permute-start(f32[17,8,128]{2,1,0:T(8,128)} %pad_maximum_fusion.11), channel_id=1, source_target_pairs={{0,32},{8,40},{16,48},{24,56},{32,64},{40,72},{48,80},{56,88},{64,... | collective-permute-start | bytes 208904 | tf_op jit(solution)/shard_map/ppermute | solution.py:22
  61.1 5.6 %collective-permute-start.14 = (bf16[128,1024]{1,0:T(8,128)(2,1)}, bf16[128,1024]{1,0:T(8,128)(2,1)}, u32[]{:S(2)}, u32[]{:S(2)}) collective-permute-start(bf16[128,1024]{1,0:T(8,128)(2,1)} %scan_output.1.own_ref), channel_id=1, source_target_pairs={{0,8},{8,0},{16,24},{24,16},{32,40},{40,32},{48,56},{56,48},{64,72... | collective-permute-start | bytes 786440 | tf_op jit(solution)/shard_map/ppermute | solution.py:27
  75.2 25.9 %all-to-all-start = ((bf16[8,2,128,256]{3,2,1,0:T(8,128)(2,1)}), bf16[8,2,128,256]{3,2,1,0:T(8,128)(2,1)S(1)}, u32[]{:S(2)}, u32[]{:S(2)}) async-start(bf16[8,2,128,256]{3,2,1,0:T(8,128)(2,1)} %project.1), calls=%async_computation | async-start | bytes 2097152 | tf_op jit(solution)/shard_map/all_to_all | solution.py:272
  101.3 3.2 %collective-permute-start.16 = (bf16[128,256]{1,0:T(8,128)(2,1)S(1)}, bf16[128,256]{1,0:T(8,128)(2,1)S(1)}, u32[]{:S(2)}, u32[]{:S(2)}) collective-permute-start(bf16[128,256]{1,0:T(8,128)(2,1)S(1)} %fusion.64), channel_id=1, source_target_pairs={{0,8},{8,0},{16,24},{24,16},{32,40},{40,32},{48,56},{56,48},{64,72... | collective-permute-start | bytes 196616 | tf_op jit(solution)/shard_map/ppermute | solution.py:27
  118.3 7.2 %collective-permute-start.21 = (bf16[24,4096]{1,0:T(8,128)(2,1)S(1)}, bf16[24,4096]{1,0:T(8,128)(2,1)S(1)}, u32[]{:S(2)}, u32[]{:S(2)}) collective-permute-start(bf16[24,4096]{1,0:T(8,128)(2,1)S(1)} %get-tuple-element.73), channel_id=1, source_target_pairs={{0,64},{8,72},{16,80},{24,88},{32,96},{40,104},{48,112},{56,120},{... | collective-permute-start | bytes 589832 | tf_op jit(solution)/shard_map/ppermute | solution.py:22
  118.6 12.2 %collective-permute-start.20 = (bf16[24,4096]{1,0:T(8,128)(2,1)S(1)}, bf16[24,4096]{1,0:T(8,128)(2,1)S(1)}, u32[]{:S(2)}, u32[]{:S(2)}) collective-permute-start(bf16[24,4096]{1,0:T(8,128)(2,1)S(1)} %get-tuple-element.73), channel_id=1, source_target_pairs={{0,32},{8,40},{16,48},{24,56},{32,64},{40,72},{48,80},{56,88},{64,... | collective-permute-start | bytes 589832 | tf_op jit(solution)/shard_map/ppermute | solution.py:22
  119.7 11.2 %collective-permute-start.22 = (bf16[24,4096]{1,0:T(8,128)(2,1)S(1)}, bf16[24,4096]{1,0:T(8,128)(2,1)S(1)}, u32[]{:S(2)}, u32[]{:S(2)}) collective-permute-start(bf16[24,4096]{1,0:T(8,128)(2,1)S(1)} %get-tuple-element.73), channel_id=1, source_target_pairs={{0,96},{8,104},{16,112},{24,120},{32,0},{40,8},{48,16},{56,24},{64... | collective-permute-start | bytes 589832 | tf_op jit(solution)/shard_map/ppermute | solution.py:22
  121.3 12.5 %collective-permute-start.18 = (bf16[24,4096]{1,0:T(8,128)(2,1)S(1)}, bf16[24,4096]{1,0:T(8,128)(2,1)S(1)}, u32[]{:S(2)}, u32[]{:S(2)}) collective-permute-start(bf16[24,4096]{1,0:T(8,128)(2,1)S(1)} %get-tuple-element.74), channel_id=1, source_target_pairs={{0,16},{8,24},{16,0},{24,8},{32,48},{40,56},{48,32},{56,40},{64,80... | collective-permute-start | bytes 589832 | tf_op jit(solution)/shard_map/ppermute | solution.py:22
  122.2 11.6 %collective-permute-start.17 = (bf16[24,4096]{1,0:T(8,128)(2,1)S(1)}, bf16[24,4096]{1,0:T(8,128)(2,1)S(1)}, u32[]{:S(2)}, u32[]{:S(2)}) collective-permute-start(bf16[24,4096]{1,0:T(8,128)(2,1)S(1)} %get-tuple-element.74), channel_id=1, source_target_pairs={{0,8},{8,16},{16,24},{24,0},{32,40},{40,48},{48,56},{56,32},{64,72... | collective-permute-start | bytes 589832 | tf_op jit(solution)/shard_map/ppermute | solution.py:22
  125.4 8.3 %collective-permute-start.19 = (bf16[24,4096]{1,0:T(8,128)(2,1)S(1)}, bf16[24,4096]{1,0:T(8,128)(2,1)S(1)}, u32[]{:S(2)}, u32[]{:S(2)}) collective-permute-start(bf16[24,4096]{1,0:T(8,128)(2,1)S(1)} %get-tuple-element.74), channel_id=1, source_target_pairs={{0,24},{8,0},{16,8},{24,16},{32,56},{40,32},{48,40},{56,48},{64,88... | collective-permute-start | bytes 589832 | tf_op jit(solution)/shard_map/ppermute | solution.py:22
  131.0 19.9 %collective-permute-start.25 = (bf16[4,24,4096]{2,1,0:T(8,128)(2,1)S(1)}, bf16[4,24,4096]{2,1,0:T(8,128)(2,1)S(1)}, u32[]{:S(2)}, u32[]{:S(2)}) collective-permute-start(bf16[4,24,4096]{2,1,0:T(8,128)(2,1)S(1)} %get-tuple-element.68), channel_id=1, source_target_pairs={{0,8},{8,16},{16,24},{24,0},{32,40},{40,48},{48,56},{56,32},{64,72... | collective-permute-start | bytes 2359304 | tf_op jit(solution)/shard_map/ppermute | solution.py:22
  131.2 19.9 %collective-permute-start.26 = (bf16[4,24,4096]{2,1,0:T(8,128)(2,1)S(1)}, bf16[4,24,4096]{2,1,0:T(8,128)(2,1)S(1)}, u32[]{:S(2)}, u32[]{:S(2)}) collective-permute-start(bf16[4,24,4096]{2,1,0:T(8,128)(2,1)S(1)} %get-tuple-element.68), channel_id=1, source_target_pairs={{0,24},{8,0},{16,8},{24,16},{32,56},{40,32},{48,40},{56,48},{64,88... | collective-permute-start | bytes 2359304 | tf_op jit(solution)/shard_map/ppermute | solution.py:22
  133.9 19.9 %collective-permute-start.23 = (bf16[4,24,4096]{2,1,0:T(8,128)(2,1)S(1)}, bf16[4,24,4096]{2,1,0:T(8,128)(2,1)S(1)}, u32[]{:S(2)}, u32[]{:S(2)}) collective-permute-start(bf16[4,24,4096]{2,1,0:T(8,128)(2,1)S(1)} %get-tuple-element.66), channel_id=1, source_target_pairs={{0,32},{8,40},{16,48},{24,56},{32,64},{40,72},{48,80},{56,88},{64,... | collective-permute-start | bytes 2359304 | tf_op jit(solution)/shard_map/ppermute | solution.py:22
  134.2 19.7 %collective-permute-start.24 = (bf16[4,24,4096]{2,1,0:T(8,128)(2,1)S(1)}, bf16[4,24,4096]{2,1,0:T(8,128)(2,1)S(1)}, u32[]{:S(2)}, u32[]{:S(2)}) collective-permute-start(bf16[4,24,4096]{2,1,0:T(8,128)(2,1)S(1)} %get-tuple-element.66), channel_id=1, source_target_pairs={{0,96},{8,104},{16,112},{24,120},{32,0},{40,8},{48,16},{56,24},{64... | collective-permute-start | bytes 2359304 | tf_op jit(solution)/shard_map/ppermute | solution.py:22
  151.0 14.2 %collective-permute-start.29 = (bf16[2,24,4096]{2,1,0:T(8,128)(2,1)S(1)}, bf16[2,24,4096]{2,1,0:T(8,128)(2,1)S(1)}, u32[]{:S(2)}, u32[]{:S(2)}) collective-permute-start(bf16[2,24,4096]{2,1,0:T(8,128)(2,1)S(1)} %slice.306), channel_id=1, source_target_pairs={{0,8},{8,16},{16,24},{24,0},{32,40},{40,48},{48,56},{56,32},{64,72... | collective-permute-start | bytes 1179656 | tf_op jit(solution)/shard_map/ppermute | solution.py:22
  151.1 14.1 %collective-permute-start.30 = (bf16[2,24,4096]{2,1,0:T(8,128)(2,1)S(1)}, bf16[2,24,4096]{2,1,0:T(8,128)(2,1)S(1)}, u32[]{:S(2)}, u32[]{:S(2)}) collective-permute-start(bf16[2,24,4096]{2,1,0:T(8,128)(2,1)S(1)} %slice.307), channel_id=1, source_target_pairs={{0,24},{8,0},{16,8},{24,16},{32,56},{40,32},{48,40},{56,48},{64,88... | collective-permute-start | bytes 1179656 | tf_op jit(solution)/shard_map/ppermute | solution.py:22
  153.8 11.5 %collective-permute-start.27 = (bf16[2,24,4096]{2,1,0:T(8,128)(2,1)S(1)}, bf16[2,24,4096]{2,1,0:T(8,128)(2,1)S(1)}, u32[]{:S(2)}, u32[]{:S(2)}) collective-permute-start(bf16[2,24,4096]{2,1,0:T(8,128)(2,1)S(1)} %slice.304), channel_id=1, source_target_pairs={{0,32},{8,40},{16,48},{24,56},{32,64},{40,72},{48,80},{56,88},{64,... | collective-permute-start | bytes 1179656 | tf_op jit(solution)/shard_map/ppermute | solution.py:22
  154.0 11.3 %collective-permute-start.28 = (bf16[2,24,4096]{2,1,0:T(8,128)(2,1)S(1)}, bf16[2,24,4096]{2,1,0:T(8,128)(2,1)S(1)}, u32[]{:S(2)}, u32[]{:S(2)}) collective-permute-start(bf16[2,24,4096]{2,1,0:T(8,128)(2,1)S(1)} %slice.305), channel_id=1, source_target_pairs={{0,96},{8,104},{16,112},{24,120},{32,0},{40,8},{48,16},{56,24},{64... | collective-permute-start | bytes 1179656 | tf_op jit(solution)/shard_map/ppermute | solution.py:22
  170.0 8.2 %collective-permute-start.40 = (bf16[2,24,4096]{2,1,0:T(8,128)(2,1)S(1)}, bf16[2,24,4096]{2,1,0:T(8,128)(2,1)S(1)}, u32[]{:S(2)}, u32[]{:S(2)}) collective-permute-start(bf16[2,24,4096]{2,1,0:T(8,128)(2,1)S(1)} %bitcast.254), channel_id=1, source_target_pairs={{0,24},{8,0},{16,8},{24,16},{32,56},{40,32},{48,40},{56,48},{64,88... | collective-permute-start | bytes 1179656 | tf_op jit(solution)/shard_map/ppermute | solution.py:22
  170.1 9.4 %collective-permute-start.31 = (bf16[2,24,4096]{2,1,0:T(8,128)(2,1)S(1)}, bf16[2,24,4096]{2,1,0:T(8,128)(2,1)S(1)}, u32[]{:S(2)}, u32[]{:S(2)}) collective-permute-start(bf16[2,24,4096]{2,1,0:T(8,128)(2,1)S(1)} %bitcast.253), channel_id=1, source_target_pairs={{0,32},{8,40},{16,48},{24,56},{32,64},{40,72},{48,80},{56,88},{64,... | collective-permute-start | bytes 1179656 | tf_op jit(solution)/shard_map/ppermute | solution.py:22
  170.2 9.4 %collective-permute-start.38 = (bf16[2,24,4096]{2,1,0:T(8,128)(2,1)S(1)}, bf16[2,24,4096]{2,1,0:T(8,128)(2,1)S(1)}, u32[]{:S(2)}, u32[]{:S(2)}) collective-permute-start(bf16[2,24,4096]{2,1,0:T(8,128)(2,1)S(1)} %bitcast.252), channel_id=1, source_target_pairs={{0,8},{8,16},{16,24},{24,0},{32,40},{40,48},{48,56},{56,32},{64,72... | collective-permute-start | bytes 1179656 | tf_op jit(solution)/shard_map/ppermute | solution.py:22
  171.5 8.1 %collective-permute-start.33 = (bf16[2,24,4096]{2,1,0:T(8,128)(2,1)S(1)}, bf16[2,24,4096]{2,1,0:T(8,128)(2,1)S(1)}, u32[]{:S(2)}, u32[]{:S(2)}) collective-permute-start(bf16[2,24,4096]{2,1,0:T(8,128)(2,1)S(1)} %bitcast.251), channel_id=1, source_target_pairs={{0,96},{8,104},{16,112},{24,120},{32,0},{40,8},{48,16},{56,24},{64... | collective-permute-start | bytes 1179656 | tf_op jit(solution)/shard_map/ppermute | solution.py:22
  180.2 16.4 %collective-permute-start.39 = (bf16[4,24,4096]{2,1,0:T(8,128)(2,1)S(1)}, bf16[4,24,4096]{2,1,0:T(8,128)(2,1)S(1)}, u32[]{:S(2)}, u32[]{:S(2)}) collective-permute-start(bf16[4,24,4096]{2,1,0:T(8,128)(2,1)S(1)} %pad_maximum_fusion.8), channel_id=1, source_target_pairs={{0,8},{8,16},{16,24},{24,0},{32,40},{40,48},{48,56},{56,32},{64,72... | collective-permute-start | bytes 2359304 | tf_op jit(solution)/shard_map/ppermute | solution.py:22
  181.4 15.4 %collective-permute-start.41 = (bf16[4,24,4096]{2,1,0:T(8,128)(2,1)S(1)}, bf16[4,24,4096]{2,1,0:T(8,128)(2,1)S(1)}, u32[]{:S(2)}, u32[]{:S(2)}) collective-permute-start(bf16[4,24,4096]{2,1,0:T(8,128)(2,1)S(1)} %pad_maximum_fusion.9), channel_id=1, source_target_pairs={{0,24},{8,0},{16,8},{24,16},{32,56},{40,32},{48,40},{56,48},{64,88... | collective-permute-start | bytes 2359304 | tf_op jit(solution)/shard_map/ppermute | solution.py:22
  183.4 17.1 %collective-permute-start.34 = (bf16[4,24,4096]{2,1,0:T(8,128)(2,1)S(1)}, bf16[4,24,4096]{2,1,0:T(8,128)(2,1)S(1)}, u32[]{:S(2)}, u32[]{:S(2)}) collective-permute-start(bf16[4,24,4096]{2,1,0:T(8,128)(2,1)S(1)} %pad_maximum_fusion.7), channel_id=1, source_target_pairs={{0,96},{8,104},{16,112},{24,120},{32,0},{40,8},{48,16},{56,24},{64... | collective-permute-start | bytes 2359304 | tf_op jit(solution)/shard_map/ppermute | solution.py:22
  186.7 15.3 %collective-permute-start.32 = (bf16[4,24,4096]{2,1,0:T(8,128)(2,1)S(1)}, bf16[4,24,4096]{2,1,0:T(8,128)(2,1)S(1)}, u32[]{:S(2)}, u32[]{:S(2)}) collective-permute-start(bf16[4,24,4096]{2,1,0:T(8,128)(2,1)S(1)} %pad_maximum_fusion.6), channel_id=1, source_target_pairs={{0,32},{8,40},{16,48},{24,56},{32,64},{40,72},{48,80},{56,88},{64,... | collective-permute-start | bytes 2359304 | tf_op jit(solution)/shard_map/ppermute | solution.py:22
  197.1 8.5 %collective-permute-start.42 = (bf16[24,4096]{1,0:T(8,128)(2,1)S(1)}, bf16[24,4096]{1,0:T(8,128)(2,1)S(1)}, u32[]{:S(2)}, u32[]{:S(2)}) collective-permute-start(bf16[24,4096]{1,0:T(8,128)(2,1)S(1)} %get-tuple-element.62), channel_id=1, source_target_pairs={{0,96},{8,104},{16,112},{24,120},{32,0},{40,8},{48,16},{56,24},{64... | collective-permute-start | bytes 589832 | tf_op jit(solution)/shard_map/ppermute | solution.py:22
  199.9 8.1 %collective-permute-start.44 = (bf16[24,4096]{1,0:T(8,128)(2,1)S(1)}, bf16[24,4096]{1,0:T(8,128)(2,1)S(1)}, u32[]{:S(2)}, u32[]{:S(2)}) collective-permute-start(bf16[24,4096]{1,0:T(8,128)(2,1)S(1)} %get-tuple-element.63), channel_id=1, source_target_pairs={{0,64},{8,72},{16,80},{24,88},{32,96},{40,104},{48,112},{56,120},{... | collective-permute-start | bytes 589832 | tf_op jit(solution)/shard_map/ppermute | solution.py:22
  199.9 10.4 %collective-permute-start.43 = (bf16[24,4096]{1,0:T(8,128)(2,1)S(1)}, bf16[24,4096]{1,0:T(8,128)(2,1)S(1)}, u32[]{:S(2)}, u32[]{:S(2)}) collective-permute-start(bf16[24,4096]{1,0:T(8,128)(2,1)S(1)} %get-tuple-element.64), channel_id=1, source_target_pairs={{0,32},{8,40},{16,48},{24,56},{32,64},{40,72},{48,80},{56,88},{64,... | collective-permute-start | bytes 589832 | tf_op jit(solution)/shard_map/ppermute | solution.py:22
  202.3 8.2 %collective-permute-start.35 = (bf16[24,4096]{1,0:T(8,128)(2,1)S(1)}, bf16[24,4096]{1,0:T(8,128)(2,1)S(1)}, u32[]{:S(2)}, u32[]{:S(2)}) collective-permute-start(bf16[24,4096]{1,0:T(8,128)(2,1)S(1)} %get-tuple-element.59), channel_id=1, source_target_pairs={{0,24},{8,0},{16,8},{24,16},{32,56},{40,32},{48,40},{56,48},{64,88... | collective-permute-start | bytes 589832 | tf_op jit(solution)/shard_map/ppermute | solution.py:22
  203.7 6.8 %collective-permute-start.37 = (bf16[24,4096]{1,0:T(8,128)(2,1)S(1)}, bf16[24,4096]{1,0:T(8,128)(2,1)S(1)}, u32[]{:S(2)}, u32[]{:S(2)}) collective-permute-start(bf16[24,4096]{1,0:T(8,128)(2,1)S(1)} %get-tuple-element.60), channel_id=1, source_target_pairs={{0,16},{8,24},{16,0},{24,8},{32,48},{40,56},{48,32},{56,40},{64,80... | collective-permute-start | bytes 589832 | tf_op jit(solution)/shard_map/ppermute | solution.py:22
  205.7 6.5 %collective-permute-start.36 = (bf16[24,4096]{1,0:T(8,128)(2,1)S(1)}, bf16[24,4096]{1,0:T(8,128)(2,1)S(1)}, u32[]{:S(2)}, u32[]{:S(2)}) collective-permute-start(bf16[24,4096]{1,0:T(8,128)(2,1)S(1)} %get-tuple-element.61), channel_id=1, source_target_pairs={{0,8},{8,16},{16,24},{24,0},{32,40},{40,48},{48,56},{56,32},{64,72... | collective-permute-start | bytes 589832 | tf_op jit(solution)/shard_map/ppermute | solution.py:22
  213.3 23.3 %all-to-all-start.2 = ((bf16[8,48,512]{2,1,0:T(8,128)(2,1)}), bf16[8,48,512]{2,1,0:T(8,128)(2,1)S(1)}, u32[]{:S(2)}, u32[]{:S(2)}) async-start(bf16[8,48,512]{2,1,0:T(8,128)(2,1)} %copy.55), calls=%async_computation.2 | async-start | bytes 786432 | tf_op jit(solution)/shard_map/all_to_all | solution.py:351
  (18 other events, 189.8 us)
where the time goes:
time: 239 us; the launch traced here: 238 us
  starting transfers between devices  81.6 us (34%)
  waiting for transfers between devices  79.1 us (33%)
  Pallas kernels  23.2 us (10%)
  matrix products  18.1 us (8%)
  local copies, waits for them, and re-layouts  12.6 us (5%)
  blocking collectives  12.5 us (5%)
  other arithmetic  9.98 us (4%)
    ppermute x42, starting transfers between devices, shift(): return lax.ppermute(value, 'seq', route)  52.4 us
    ppermute x42, waiting for transfers between devices, shift(): return lax.ppermute(value, 'seq', route)  50.1 us
    all_to_all x1, starting transfers between devices, local(): returned = lax.all_to_all(summed, 'exp', split_axis=0, concat_axis=0)  15.2 us
    all_to_all x1, waiting for transfers between devices, project(): partial = lax.all_to_all(partial, 'exp', split_axis=0, concat_axis=0)  13.5 us
    all_to_all x1, blocking collectives, local(): lax.all_to_all(outgoing, 'exp', split_axis=0, concat_axis=2, tiled=True)[0]  12.5 us
    all_to_all x1, starting transfers between devices, project(): partial = lax.all_to_all(partial, 'exp', split_axis=0, concat_axis=0)  10.8 us
    pallas_call x1, Pallas kernels, mixer(): pl.pallas_call(second_pass, out_shape=jax.ShapeDtypeStruct((tokens, chann...  8.46 us
    all_to_all x1, waiting for transfers between devices, local(): returned = lax.all_to_all(summed, 'exp', split_axis=0, concat_axis=0)  8.09 us
  transfers between devices with their start and end apart: 47, of which 24 were waited for; matrix products, arithmetic and copies ran while one was open for 11% of the time, Pallas kernels for 7%

commit v1 on v0

--- a/solution.py
+++ b/solution.py
@@ -224,28 +224,29 @@
     return mixed, (first, second)
 
 
-def project_kernel(place_ref, own_ref, other_ref, *refs):
+def project_kernel(place_ref, *refs):
     count = SIDE + 2
-    out_ref, rows, first, second, semaphores = refs[count:]
+    out_ref, first, second, semaphores = refs[-4:]
+    rows_ref, fixed = refs[count], refs[count + 1 : -4]
     targets = [first.at[i] for i in range(SIDE)] + [second.at[j] for j in range(2)]
     fetch(refs[:count], targets, semaphores)
-    tokens = own_ref.shape[0]
-    rows[:tokens] = own_ref[...]
-    rows[tokens:] = other_ref[...]
     split = first.shape[2]
     y, side = place_ref[0], place_ref[1]
-
-    def one(step, carry):
-        i, j = step // 2, step % 2
-        owner = lax.rem(y - i + SIDE, SIDE) * 2 + lax.rem(side + j, 2)
-        total = jnp.dot(rows[:, :split], first[i, j], preferred_element_type=F32)
-        total += jnp.dot(rows[:, split:], second[j, i], preferred_element_type=F32)
-        total = total.astype(BF16)
-        out_ref[owner, 0] = total[:tokens]
-        out_ref[owner, 1] = total[tokens:]
+    if fixed:
+        out_ref[:, 0] = fixed[0][...]
+
+    def one(i, carry):
+        for j in range(2):
+            owner = lax.rem(y - i + SIDE, SIDE) * 2 + lax.rem(side + j, 2)
+            total = jnp.dot(rows_ref[:, :split], first[i, j], preferred_element_type=F32)
+            total += jnp.dot(rows_ref[:, split:], second[j, i], preferred_element_type=F32)
+            if fixed:
+                out_ref[owner, 1] = total.astype(BF16)
+            else:
+                out_ref[owner] = total.astype(BF16)
         return carry
 
-    lax.fori_loop(0, 2 * SIDE, one, 0)
+    lax.fori_loop(0, SIDE, one, 0)
 
 
 def project(mixed, weights):
@@ -255,20 +256,27 @@
     place = jnp.stack([index // SIDE, index % SIDE // 2]).astype(jnp.int32)
     vmem = pl.BlockSpec(memory_space=pltpu.VMEM)
     stay = pl.BlockSpec(memory_space=pltpu.HBM)
-    partial = pl.pallas_call(
-        project_kernel,
-        out_shape=jax.ShapeDtypeStruct((2 * SIDE, 2, tokens, columns), BF16),
-        in_specs=[pl.BlockSpec(memory_space=pltpu.SMEM)] + [vmem] * 2 + [stay] * (SIDE + 2),
-        out_specs=vmem,
-        scratch_shapes=[
-            pltpu.VMEM((2 * tokens, mixed.shape[1]), BF16),
-            pltpu.VMEM((SIDE, *first[0].shape), BF16),
-            pltpu.VMEM((2, *second[0].shape), BF16),
-            pltpu.SemaphoreType.DMA((SIDE + 2,)),
-        ],
-        compiler_params=pltpu.CompilerParams(vmem_limit_bytes=58 << 20),
-        name="project",
-    )(place, mixed, partner(mixed), *first, *second)
+
+    def call(shape, *operands):
+        return pl.pallas_call(
+            project_kernel,
+            out_shape=jax.ShapeDtypeStruct(shape, BF16),
+            in_specs=[pl.BlockSpec(memory_space=pltpu.SMEM)]
+            + [stay] * (SIDE + 2)
+            + [vmem] * len(operands),
+            out_specs=vmem,
+            scratch_shapes=[
+                pltpu.VMEM((SIDE, *first[0].shape), BF16),
+                pltpu.VMEM((2, *second[0].shape), BF16),
+                pltpu.SemaphoreType.DMA((SIDE + 2,)),
+            ],
+            compiler_params=pltpu.CompilerParams(vmem_limit_bytes=58 << 20),
+            name="project",
+        )(place, *first, *second, *operands)
+
+    other = partner(mixed)
+    own = call((2 * SIDE, tokens, columns), mixed)
+    partial = call((2 * SIDE, 2, tokens, columns), other, own)
     partial = lax.all_to_all(partial, "exp", split_axis=0, concat_axis=0)
     total = jnp.sum(partial.astype(F32), axis=0)
     other = partner(total[1].astype(BF16)).astype(F32)

time: 239 us -> 236 us (0.987)
  Pallas kernels: 23.2 us -> 27.3 us
  other arithmetic: 9.98 us -> 6.61 us
  waiting for transfers between devices: 79.1 us -> 76.1 us
    ppermute x2, waiting for transfers between devices: 7.36 us -> 1.95 us  [partner(): return lax.ppermute(value, 'seq', [(i, i ^ 1) for i in cells])]
    pallas_call x1 -> x2, Pallas kernels: 7.41 us -> 11.5 us  [call(): pl.pallas_call(project_kernel, out_shape=jax.ShapeDtypeStruct(shape, BF16...]
    ppermute x42, waiting for transfers between devices: 50.1 us -> 52.5 us  [shift(): return lax.ppermute(value, 'seq', route)]
    unnamed x45 -> x49, local copies, waits for them, and re-layouts: 7.77 us -> 7.79 us
  transfers between devices with their start and end apart: 47 -> 47, of which waited for: 24 -> 22; matrix products, arithmetic and copies ran while one was open for 11% -> 10% of each run, Pallas kernels for 7% -> 9%
where the time goes in v1:
time: 236 us; the launch traced here: 235 us
  starting transfers between devices  81.5 us (35%)
  waiting for transfers between devices  76.1 us (32%)
  Pallas kernels  27.3 us (12%)
  matrix products  18.1 us (8%)
  local copies, waits for them, and re-layouts  12.7 us (5%)
  blocking collectives  12.5 us (5%)
  other arithmetic  6.61 us (3%)
    ppermute x42, starting transfers between devices, shift(): return lax.ppermute(value, 'seq', route)  53.2 us
    ppermute x42, waiting for transfers between devices, shift(): return lax.ppermute(value, 'seq', route)  52.5 us
    all_to_all x1, starting transfers between devices, local(): returned = lax.all_to_all(summed, 'exp', split_axis=0, concat_axis=0)  15.2 us
    all_to_all x1, waiting for transfers between devices, project(): partial = lax.all_to_all(partial, 'exp', split_axis=0, concat_axis=0)  13.5 us
    all_to_all x1, blocking collectives, local(): lax.all_to_all(outgoing, 'exp', split_axis=0, concat_axis=2, tiled=True)[0]  12.5 us
    pallas_call x2, Pallas kernels, call(): pl.pallas_call(project_kernel, out_shape=jax.ShapeDtypeStruct(shape, BF16...  11.5 us
    all_to_all x1, starting transfers between devices, project(): partial = lax.all_to_all(partial, 'exp', split_axis=0, concat_axis=0)  9.2 us
    pallas_call x1, Pallas kernels, mixer(): pl.pallas_call(second_pass, out_shape=jax.ShapeDtypeStruct((tokens, chann...  8.49 us
  transfers between devices with their start and end apart: 47, of which 22 were waited for; matrix products, arithmetic and copies ran while one was open for 10% of the time, Pallas kernels for 9%

profile of v1, /device:TPU:1, one launch (start us, length us, event | category | flops | bytes accessed | tf_op | source)
XLA Modules:
  0.0 235.4 jit_solution(3271710570892452952)
XLA Ops:
  1.0 3.7 %collective-permute-start = (bf16[448,256]{1,0:T(8,128)(2,1)S(1)}, bf16[448,256]{1,0:T(8,128)(2,1)S(1)}, u32[]{:S(2)}, u32[]{:S(2)}) collective-permute-start(bf16[448,256]{1,0:T(8,128)(2,1)S(1)} %get-tuple-element.70), channel_id=1, source_target_pairs={{0,16},{8,24},{16,0},{24,8},{32,48},{40,56},{48,32},{56,40},{64,80... | collective-permute-start | bytes 688136 | tf_op jit(solution)/shard_map/ppermute | solution.py:22
  5.6 2.8 %collective-permute-start.4 = (bf16[576,256]{1,0:T(8,128)(2,1)S(1)}, bf16[576,256]{1,0:T(8,128)(2,1)S(1)}, u32[]{:S(2)}, u32[]{:S(2)}) collective-permute-start(bf16[576,256]{1,0:T(8,128)(2,1)S(1)} %slice.228), channel_id=1, source_target_pairs={{0,96},{8,104},{16,112},{24,120},{32,0},{40,8},{48,16},{56,24},{64... | collective-permute-start | bytes 884744 | tf_op jit(solution)/shard_map/ppermute | solution.py:22
  10.2 2.2 collective-permute-start.1
  15.4 2.1 collective-permute-start.10
  18.9 7.3 %scan_state.1 = (f32[128,8,128]{2,1,0:T(8,128)}, f32[128,8,128]{2,1,0:T(8,128)}, f32[17,8,128]{2,1,0:T(8,128)}) custom-call(bf16[128,1024]{1,0:T(8,128)(2,1)} %x_hbm.1, bf16[128,1024]{1,0:T(8,128)(2,1)} %dt_hbm, bf16[8,1024]{1,0:T(8,128)(2,1)} %copy-done.11, f32[1,1024]{1,0:T(1,128)} %bitcast.267, f32[4,1024]{1,0:T(4,128)} %bitcast.266, ...), custom_call_target="tpu_custom_call" | custom-call | tf_op jit(solution)/shard_map/scan_state/pallas_call | solution.py:202
  26.4 2.0 collective-permute-start.7
  29.2 1.5 collective-permute-done.7
  31.4 2.2 collective-permute-done.6
  35.3 7.4 %collective-permute-done.8.refs_1_ = bf16[2,448,256]{2,1,0:T(8,128)(2,1)S(1)} collective-permute-done((bf16[2,448,256]{2,1,0:T(8,128)(2,1)S(1)}, bf16[2,448,256]{2,1,0:T(8,128)(2,1)S(1)}, u32[]{:S(2)}, u32[]{:S(2)}) %collective-permute-start.8) | collective-permute-done | bytes 458784 | tf_op jit(solution)/shard_map/ppermute | solution.py:22
  44.8 1.5 collective-permute-start.14
  46.3 2.1 collective-permute-done.13
  48.4 2.5 %collective-permute-done.12 = f32[17,8,128]{2,1,0:T(8,128)S(1)} collective-permute-done((f32[17,8,128]{2,1,0:T(8,128)S(1)}, f32[17,8,128]{2,1,0:T(8,128)S(1)}, u32[]{:S(2)}, u32[]{:S(2)}) %collective-permute-start.12) | collective-permute-done | bytes 69664 | tf_op jit(solution)/shard_map/ppermute | solution.py:22
  51.7 8.5 %scan_output.1.refs_6_ = bf16[128,1024]{1,0:T(8,128)(2,1)} custom-call(f32[128,8,128]{2,1,0:T(8,128)} %get-tuple-element.36.step_hbm, f32[128,8,128]{2,1,0:T(8,128)} %get-tuple-element.37.act_hbm, bf16[128,1024]{1,0:T(8,128)(2,1)} %gate_hbm.1, f32[16,8,128]{2,1,0:T(8,128)} %fusion.67.enter_ref, f32[16,8,128]{2,1,0:T(8,128)} %bitcast.240, ...), custom_call_target="tpu_custom_call" | custom-call | tf_op jit(solution)/shard_map/scan_output/pallas_call | solution.py:215
  62.3 5.5 %project.2.refs_7_ = bf16[8,128,256]{2,1,0:T(8,128)(2,1)} custom-call(s32[2]{0:T(128)} %pad_add_fusion.place_ref, bf16[2,448,256]{2,1,0:T(8,128)(2,1)} %copy-done.2, bf16[2,448,256]{2,1,0:T(8,128)(2,1)} %copy-done.5, bf16[2,448,256]{2,1,0:T(8,128)(2,1)} %copy-done.4, bf16[2,448,256]{2,1,0:T(8,128)(2,1)} %copy-done.3, bf16[4,576,256]{2,1,0:T(8,128)(2,1)} %copy-done, ...), custom_call_target="tpu_custom_call" | custom-call | tf_op jit(solution)/shard_map/project/pallas_call | solution.py:261
  68.5 5.9 %project.3 = bf16[8,2,128,256]{3,2,1,0:T(8,128)(2,1)} custom-call(s32[2]{0:T(128)} %pad_add_fusion.place_ref, bf16[2,448,256]{2,1,0:T(8,128)(2,1)} %copy-done.2, bf16[2,448,256]{2,1,0:T(8,128)(2,1)} %copy-done.5, bf16[2,448,256]{2,1,0:T(8,128)(2,1)} %copy-done.4, bf16[2,448,256]{2,1,0:T(8,128)(2,1)} %copy-done.3, bf16[4,576,256]{2,1,0:T(8,128)(2,1)} %copy-done, ...), custom_call_target="tpu_custom_call" | custom-call | tf_op jit(solution)/shard_map/project/pallas_call | solution.py:261
  74.5 9.2 %all-to-all-start = ((bf16[8,2,128,256]{3,2,1,0:T(8,128)(2,1)}), bf16[8,2,128,256]{3,2,1,0:T(8,128)(2,1)S(1)}, u32[]{:S(2)}, u32[]{:S(2)}) async-start(bf16[8,2,128,256]{3,2,1,0:T(8,128)(2,1)} %project.3), calls=%async_computation | async-start | bytes 2097152 | tf_op jit(solution)/shard_map/all_to_all | solution.py:280
  85.2 13.5 %all-to-all-done = bf16[8,2,128,256]{3,2,1,0:T(8,128)(2,1)S(1)} async-done(((bf16[8,2,128,256]{3,2,1,0:T(8,128)(2,1)}), bf16[8,2,128,256]{3,2,1,0:T(8,128)(2,1)S(1)}, u32[]{:S(2)}, u32[]{:S(2)}) %all-to-all-start) | async-done | bytes 1048608 | tf_op jit(solution)/shard_map/all_to_all | solution.py:280
  100.2 1.9 collective-permute-done.16
  102.4 12.5 %all_to_all.19 = bf16[8,48,512]{2,1,0:T(8,128)(2,1)S(1)} all-to-all(bf16[8,48,512]{2,1,0:T(8,128)(2,1)S(1)} %bitcast.245), channel_id=1, replica_groups=mesh['seq'=16,'exp'=8] {'exp'}, dimensions={0} | all-to-all | bytes 786432 | tf_op jit(solution)/shard_map/all_to_all | solution.py:331
  116.4 2.1 collective-permute-start.20
  119.1 3.6 %collective-permute-start.18 = (bf16[24,4096]{1,0:T(8,128)(2,1)S(1)}, bf16[24,4096]{1,0:T(8,128)(2,1)S(1)}, u32[]{:S(2)}, u32[]{:S(2)}) collective-permute-start(bf16[24,4096]{1,0:T(8,128)(2,1)S(1)} %get-tuple-element.74), channel_id=1, source_target_pairs={{0,16},{8,24},{16,0},{24,8},{32,48},{40,56},{48,32},{56,40},{64,80... | collective-permute-start | bytes 589832 | tf_op jit(solution)/shard_map/ppermute | solution.py:22
  123.0 2.4 %collective-permute-start.19 = (bf16[24,4096]{1,0:T(8,128)(2,1)S(1)}, bf16[24,4096]{1,0:T(8,128)(2,1)S(1)}, u32[]{:S(2)}, u32[]{:S(2)}) collective-permute-start(bf16[24,4096]{1,0:T(8,128)(2,1)S(1)} %get-tuple-element.74), channel_id=1, source_target_pairs={{0,24},{8,0},{16,8},{24,16},{32,56},{40,32},{48,40},{56,48},{64,88... | collective-permute-start | bytes 589832 | tf_op jit(solution)/shard_map/ppermute | solution.py:22
  125.4 3.1 %collective-permute-done.20 = bf16[24,4096]{1,0:T(8,128)(2,1)S(1)} collective-permute-done((bf16[24,4096]{1,0:T(8,128)(2,1)S(1)}, bf16[24,4096]{1,0:T(8,128)(2,1)S(1)}, u32[]{:S(2)}, u32[]{:S(2)}) %collective-permute-start.20) | collective-permute-done | bytes 196640 | tf_op jit(solution)/shard_map/ppermute | solution.py:22
  129.7 1.6 collective-permute-start.26
  132.0 2.3 collective-permute-start.24
  134.4 1.4 fusion.16
  137.2 1.4 fusion.38
  140.7 7.8 %collective-permute-done.25 = bf16[4,24,4096]{2,1,0:T(8,128)(2,1)S(1)} collective-permute-done((bf16[4,24,4096]{2,1,0:T(8,128)(2,1)S(1)}, bf16[4,24,4096]{2,1,0:T(8,128)(2,1)S(1)}, u32[]{:S(2)}, u32[]{:S(2)}) %collective-permute-start.25) | collective-permute-done | bytes 786464 | tf_op jit(solution)/shard_map/ppermute | solution.py:22
  149.5 1.9 collective-permute-start.30
  151.9 2.3 collective-permute-start.28
  154.7 2.6 %fusion.14 = f32[384,768]{1,0:T(8,128)S(1)} fusion(bf16[384,4096]{1,0:T(8,128)(2,1)S(1)} %bitcast.228, bf16[1,4096,768]{2,1,0:T(8,128)(2,1)S(1)} %bitcast.271), kind=kOutput, calls=%fused_computation.14 | convolution fusion | flops 2415919104 | bytes 10616832 | tf_op jit(solution)/shard_map/dot_general | solution.py:342
  157.3 2.7 %multiply_convert_fusion = bf16[384,768]{1,0:T(8,128)(2,1)S(1)} fusion(f32[384,768]{1,0:T(8,128)S(1)} %fusion.14, bf16[384,4096]{1,0:T(8,128)(2,1)S(1)} %bitcast.229, bf16[1,4096,768]{2,1,0:T(8,128)(2,1)S(1)} %bitcast.273), kind=kOutput, calls=%fused_computation.35 | convolution fusion | flops 2417688576 | bytes 11206656 | tf_op jit(solution)/shard_map/dot_general | solution.py:343
  159.9 2.8 %fusion.18 = bf16[384,4096]{1,0:T(8,128)(2,1)S(1)} fusion(bf16[384,768]{1,0:T(8,128)(2,1)S(1)} %multiply_convert_fusion, bf16[1,768,4096]{2,1,0:T(8,128)(2,1)S(1)} %bitcast.275), kind=kOutput, calls=%fused_computation.18 | convolution fusion | flops 2417491968 | bytes 10027008 | tf_op jit(solution)/shard_map/dot_general | solution.py:345
  163.1 1.4 fusion.12
  164.6 1.4 fusion.35
  169.1 2.7 %collective-permute-start.33 = (bf16[2,24,4096]{2,1,0:T(8,128)(2,1)S(1)}, bf16[2,24,4096]{2,1,0:T(8,128)(2,1)S(1)}, u32[]{:S(2)}, u32[]{:S(2)}) collective-permute-start(bf16[2,24,4096]{2,1,0:T(8,128)(2,1)S(1)} %bitcast.251), channel_id=1, source_target_pairs={{0,96},{8,104},{16,112},{24,120},{32,0},{40,8},{48,16},{56,24},{64... | collective-permute-start | bytes 1179656 | tf_op jit(solution)/shard_map/ppermute | solution.py:22
  171.9 3.9 %collective-permute-done.40 = bf16[2,24,4096]{2,1,0:T(8,128)(2,1)S(1)} collective-permute-done((bf16[2,24,4096]{2,1,0:T(8,128)(2,1)S(1)}, bf16[2,24,4096]{2,1,0:T(8,128)(2,1)S(1)}, u32[]{:S(2)}, u32[]{:S(2)}) %collective-permute-start.40) | collective-permute-done | bytes 393248 | tf_op jit(solution)/shard_map/ppermute | solution.py:22
  179.0 1.7 collective-permute-start.41
  180.7 3.5 %collective-permute-start.34 = (bf16[4,24,4096]{2,1,0:T(8,128)(2,1)S(1)}, bf16[4,24,4096]{2,1,0:T(8,128)(2,1)S(1)}, u32[]{:S(2)}, u32[]{:S(2)}) collective-permute-start(bf16[4,24,4096]{2,1,0:T(8,128)(2,1)S(1)} %pad_maximum_fusion.7), channel_id=1, source_target_pairs={{0,96},{8,104},{16,112},{24,120},{32,0},{40,8},{48,16},{56,24},{64... | collective-permute-start | bytes 2359304 | tf_op jit(solution)/shard_map/ppermute | solution.py:22
  184.3 9.3 %collective-permute-done.39 = bf16[4,24,4096]{2,1,0:T(8,128)(2,1)S(1)} collective-permute-done((bf16[4,24,4096]{2,1,0:T(8,128)(2,1)S(1)}, bf16[4,24,4096]{2,1,0:T(8,128)(2,1)S(1)}, u32[]{:S(2)}, u32[]{:S(2)}) %collective-permute-start.39) | collective-permute-done | bytes 786464 | tf_op jit(solution)/shard_map/ppermute | solution.py:22
  194.7 2.8 %collective-permute-start.42 = (bf16[24,4096]{1,0:T(8,128)(2,1)S(1)}, bf16[24,4096]{1,0:T(8,128)(2,1)S(1)}, u32[]{:S(2)}, u32[]{:S(2)}) collective-permute-start(bf16[24,4096]{1,0:T(8,128)(2,1)S(1)} %get-tuple-element.62), channel_id=1, source_target_pairs={{0,96},{8,104},{16,112},{24,120},{32,0},{40,8},{48,16},{56,24},{64... | collective-permute-start | bytes 589832 | tf_op jit(solution)/shard_map/ppermute | solution.py:22
  199.9 1.4 collective-permute-start.35
  201.3 1.9 collective-permute-done.42
  203.2 2.3 collective-permute-done.44
  205.5 2.4 %collective-permute-done.43 = bf16[24,4096]{1,0:T(8,128)(2,1)S(1)} collective-permute-done((bf16[24,4096]{1,0:T(8,128)(2,1)S(1)}, bf16[24,4096]{1,0:T(8,128)(2,1)S(1)}, u32[]{:S(2)}, u32[]{:S(2)}) %collective-permute-start.43) | collective-permute-done | bytes 196640 | tf_op jit(solution)/shard_map/ppermute | solution.py:22
  208.1 1.6 collective-permute-done.36
  210.8 15.2 %all-to-all-start.2 = ((bf16[8,48,512]{2,1,0:T(8,128)(2,1)}), bf16[8,48,512]{2,1,0:T(8,128)(2,1)S(1)}, u32[]{:S(2)}, u32[]{:S(2)}) async-start(bf16[8,48,512]{2,1,0:T(8,128)(2,1)} %copy.55), calls=%async_computation.2 | async-start | bytes 786432 | tf_op jit(solution)/shard_map/all_to_all | solution.py:359
  226.1 8.1 %all-to-all-done.2 = bf16[8,48,512]{2,1,0:T(8,128)(2,1)S(1)} async-done(((bf16[8,48,512]{2,1,0:T(8,128)(2,1)}), bf16[8,48,512]{2,1,0:T(8,128)(2,1)S(1)}, u32[]{:S(2)}, u32[]{:S(2)}) %all-to-all-start.2) | async-done | bytes 393248 | tf_op jit(solution)/shard_map/all_to_all | solution.py:359
  (176 shorter events, 42.6 us)
Async XLA Ops:
  1.0 14.3 %collective-permute-start = (bf16[448,256]{1,0:T(8,128)(2,1)S(1)}, bf16[448,256]{1,0:T(8,128)(2,1)S(1)}, u32[]{:S(2)}, u32[]{:S(2)}) collective-permute-start(bf16[448,256]{1,0:T(8,128)(2,1)S(1)} %get-tuple-element.70), channel_id=1, source_target_pairs={{0,16},{8,24},{16,0},{24,8},{32,48},{40,56},{48,32},{56,40},{64,80... | collective-permute-start | bytes 688136 | tf_op jit(solution)/shard_map/ppermute | solution.py:22
  5.6 20.6 %collective-permute-start.4 = (bf16[576,256]{1,0:T(8,128)(2,1)S(1)}, bf16[576,256]{1,0:T(8,128)(2,1)S(1)}, u32[]{:S(2)}, u32[]{:S(2)}) collective-permute-start(bf16[576,256]{1,0:T(8,128)(2,1)S(1)} %slice.228), channel_id=1, source_target_pairs={{0,96},{8,104},{16,112},{24,120},{32,0},{40,8},{48,16},{56,24},{64... | collective-permute-start | bytes 884744 | tf_op jit(solution)/shard_map/ppermute | solution.py:22
  8.4 17.8 %collective-permute-start.3 = (bf16[576,256]{1,0:T(8,128)(2,1)S(1)}, bf16[576,256]{1,0:T(8,128)(2,1)S(1)}, u32[]{:S(2)}, u32[]{:S(2)}) collective-permute-start(bf16[576,256]{1,0:T(8,128)(2,1)S(1)} %slice.228), channel_id=1, source_target_pairs={{0,64},{8,72},{16,80},{24,88},{32,96},{40,104},{48,112},{56,120},{... | collective-permute-start | bytes 884744 | tf_op jit(solution)/shard_map/ppermute | solution.py:22
  8.8 17.7 %collective-permute-start.2 = (bf16[576,256]{1,0:T(8,128)(2,1)S(1)}, bf16[576,256]{1,0:T(8,128)(2,1)S(1)}, u32[]{:S(2)}, u32[]{:S(2)}) collective-permute-start(bf16[576,256]{1,0:T(8,128)(2,1)S(1)} %slice.228), channel_id=1, source_target_pairs={{0,32},{8,40},{16,48},{24,56},{32,64},{40,72},{48,80},{56,88},{64,... | collective-permute-start | bytes 884744 | tf_op jit(solution)/shard_map/ppermute | solution.py:22
  10.2 7.3 %collective-permute-start.1 = (bf16[8,1024]{1,0:T(8,128)(2,1)S(1)}, bf16[8,1024]{1,0:T(8,128)(2,1)S(1)}, u32[]{:S(2)}, u32[]{:S(2)}) collective-permute-start(bf16[8,1024]{1,0:T(8,128)(2,1)S(1)} %slice.227), channel_id=1, source_target_pairs={{0,8},{8,16},{16,24},{24,32},{32,40},{40,48},{48,56},{56,64},{64,7... | collective-permute-start | bytes 49160 | tf_op jit(solution)/shard_map/ppermute | solution.py:190
  15.4 19.9 %collective-permute-start.10 = (bf16[2,448,256]{2,1,0:T(8,128)(2,1)S(1)}, bf16[2,448,256]{2,1,0:T(8,128)(2,1)S(1)}, u32[]{:S(2)}, u32[]{:S(2)}) collective-permute-start(bf16[2,448,256]{2,1,0:T(8,128)(2,1)S(1)} %pad_maximum_fusion.10.refs_0_), channel_id=1, source_target_pairs={{0,96},{8,104},{16,112},{24,120},{32,0},{40,8},{48,16},{56,24},{64... | collective-permute-start | bytes 1376264 | tf_op jit(solution)/shard_map/ppermute | solution.py:22
  17.4 17.8 %collective-permute-start.9 = (bf16[2,448,256]{2,1,0:T(8,128)(2,1)S(1)}, bf16[2,448,256]{2,1,0:T(8,128)(2,1)S(1)}, u32[]{:S(2)}, u32[]{:S(2)}) collective-permute-start(bf16[2,448,256]{2,1,0:T(8,128)(2,1)S(1)} %pad_maximum_fusion.10.refs_0_), channel_id=1, source_target_pairs={{0,64},{8,72},{16,80},{24,88},{32,96},{40,104},{48,112},{56,120},{... | collective-permute-start | bytes 1376264 | tf_op jit(solution)/shard_map/ppermute | solution.py:22
  26.4 4.3 %collective-permute-start.7 = (f32[17,8,128]{2,1,0:T(8,128)}, f32[17,8,128]{2,1,0:T(8,128)S(1)}, u32[]{:S(2)}, u32[]{:S(2)}) collective-permute-start(f32[17,8,128]{2,1,0:T(8,128)} %get-tuple-element.24), channel_id=1, source_target_pairs={{0,24},{8,0},{16,8},{24,16},{32,56},{40,32},{48,40},{56,48},{64,88... | collective-permute-start | bytes 208904 | tf_op jit(solution)/shard_map/ppermute | solution.py:22
  28.4 5.2 %collective-permute-start.6 = (f32[17,8,128]{2,1,0:T(8,128)}, f32[17,8,128]{2,1,0:T(8,128)S(1)}, u32[]{:S(2)}, u32[]{:S(2)}) collective-permute-start(f32[17,8,128]{2,1,0:T(8,128)} %get-tuple-element.24), channel_id=1, source_target_pairs={{0,16},{8,24},{16,0},{24,8},{32,48},{40,56},{48,32},{56,40},{64,80... | collective-permute-start | bytes 208904 | tf_op jit(solution)/shard_map/ppermute | solution.py:22
  28.9 5.5 %collective-permute-start.5 = (f32[17,8,128]{2,1,0:T(8,128)}, f32[17,8,128]{2,1,0:T(8,128)S(1)}, u32[]{:S(2)}, u32[]{:S(2)}) collective-permute-start(f32[17,8,128]{2,1,0:T(8,128)} %get-tuple-element.24), channel_id=1, source_target_pairs={{0,8},{8,16},{16,24},{24,0},{32,40},{40,48},{48,56},{56,32},{64,72... | collective-permute-start | bytes 208904 | tf_op jit(solution)/shard_map/ppermute | solution.py:22
  29.2 31.3 %copy-start = (bf16[4,576,256]{2,1,0:T(8,128)(2,1)}, bf16[4,576,256]{2,1,0:T(8,128)(2,1)S(1)}, u32[]{:S(2)}) copy-start(bf16[4,576,256]{2,1,0:T(8,128)(2,1)S(1)} %pad_maximum_fusion.3.refs_4_) | copy-start | bytes 3538948
  30.8 11.9 %collective-permute-start.8 = (bf16[2,448,256]{2,1,0:T(8,128)(2,1)S(1)}, bf16[2,448,256]{2,1,0:T(8,128)(2,1)S(1)}, u32[]{:S(2)}, u32[]{:S(2)}) collective-permute-start(bf16[2,448,256]{2,1,0:T(8,128)(2,1)S(1)} %pad_maximum_fusion.10.refs_0_), channel_id=1, source_target_pairs={{0,32},{8,40},{16,48},{24,56},{32,64},{40,72},{48,80},{56,88},{64,... | collective-permute-start | bytes 1376264 | tf_op jit(solution)/shard_map/ppermute | solution.py:22
  34.5 26.7 %collective-permute-start.11 = (bf16[4,576,256]{2,1,0:T(8,128)(2,1)S(1)}, bf16[4,576,256]{2,1,0:T(8,128)(2,1)S(1)}, u32[]{:S(2)}, u32[]{:S(2)}) collective-permute-start(bf16[4,576,256]{2,1,0:T(8,128)(2,1)S(1)} %pad_maximum_fusion.3.refs_4_), channel_id=1, source_target_pairs={{0,16},{8,24},{16,0},{24,8},{32,48},{40,56},{48,32},{56,40},{64,80... | collective-permute-start | bytes 3538952 | tf_op jit(solution)/shard_map/ppermute | solution.py:22
  43.5 5.0 %collective-permute-start.13 = (f32[17,8,128]{2,1,0:T(8,128)S(1)}, f32[17,8,128]{2,1,0:T(8,128)S(1)}, u32[]{:S(2)}, u32[]{:S(2)}) collective-permute-start(f32[17,8,128]{2,1,0:T(8,128)S(1)} %pad_maximum_fusion.11), channel_id=1, source_target_pairs={{0,64},{8,72},{16,80},{24,88},{32,96},{40,104},{48,112},{56,120},{... | collective-permute-start | bytes 208904 | tf_op jit(solution)/shard_map/ppermute | solution.py:22
  44.8 6.2 %collective-permute-start.14 = (f32[17,8,128]{2,1,0:T(8,128)S(1)}, f32[17,8,128]{2,1,0:T(8,128)S(1)}, u32[]{:S(2)}, u32[]{:S(2)}) collective-permute-start(f32[17,8,128]{2,1,0:T(8,128)S(1)} %pad_maximum_fusion.11), channel_id=1, source_target_pairs={{0,96},{8,104},{16,112},{24,120},{32,0},{40,8},{48,16},{56,24},{64... | collective-permute-start | bytes 208904 | tf_op jit(solution)/shard_map/ppermute | solution.py:22
  46.3 4.7 %collective-permute-start.12 = (f32[17,8,128]{2,1,0:T(8,128)S(1)}, f32[17,8,128]{2,1,0:T(8,128)S(1)}, u32[]{:S(2)}, u32[]{:S(2)}) collective-permute-start(f32[17,8,128]{2,1,0:T(8,128)S(1)} %pad_maximum_fusion.11), channel_id=1, source_target_pairs={{0,32},{8,40},{16,48},{24,56},{32,64},{40,72},{48,80},{56,88},{64,... | collective-permute-start | bytes 208904 | tf_op jit(solution)/shard_map/ppermute | solution.py:22
  60.2 7.7 %collective-permute-start.15 = (bf16[128,1024]{1,0:T(8,128)(2,1)}, bf16[128,1024]{1,0:T(8,128)(2,1)S(1)}, u32[]{:S(2)}, u32[]{:S(2)}) collective-permute-start(bf16[128,1024]{1,0:T(8,128)(2,1)} %scan_output.1.refs_6_), channel_id=1, source_target_pairs={{0,8},{8,0},{16,24},{24,16},{32,40},{40,32},{48,56},{56,48},{64,72... | collective-permute-start | bytes 786440 | tf_op jit(solution)/shard_map/ppermute | solution.py:27
  74.5 24.3 %all-to-all-start = ((bf16[8,2,128,256]{3,2,1,0:T(8,128)(2,1)}), bf16[8,2,128,256]{3,2,1,0:T(8,128)(2,1)S(1)}, u32[]{:S(2)}, u32[]{:S(2)}) async-start(bf16[8,2,128,256]{3,2,1,0:T(8,128)(2,1)} %project.3), calls=%async_computation | async-start | bytes 2097152 | tf_op jit(solution)/shard_map/all_to_all | solution.py:280
  98.9 3.2 %collective-permute-start.16 = (bf16[128,256]{1,0:T(8,128)(2,1)S(1)}, bf16[128,256]{1,0:T(8,128)(2,1)S(1)}, u32[]{:S(2)}, u32[]{:S(2)}) collective-permute-start(bf16[128,256]{1,0:T(8,128)(2,1)S(1)} %fusion.64), channel_id=1, source_target_pairs={{0,8},{8,0},{16,24},{24,16},{32,40},{40,32},{48,56},{56,48},{64,72... | collective-permute-start | bytes 196616 | tf_op jit(solution)/shard_map/ppermute | solution.py:27
  115.8 7.2 %collective-permute-start.21 = (bf16[24,4096]{1,0:T(8,128)(2,1)S(1)}, bf16[24,4096]{1,0:T(8,128)(2,1)S(1)}, u32[]{:S(2)}, u32[]{:S(2)}) collective-permute-start(bf16[24,4096]{1,0:T(8,128)(2,1)S(1)} %get-tuple-element.73), channel_id=1, source_target_pairs={{0,64},{8,72},{16,80},{24,88},{32,96},{40,104},{48,112},{56,120},{... | collective-permute-start | bytes 589832 | tf_op jit(solution)/shard_map/ppermute | solution.py:22
  116.4 12.0 %collective-permute-start.20 = (bf16[24,4096]{1,0:T(8,128)(2,1)S(1)}, bf16[24,4096]{1,0:T(8,128)(2,1)S(1)}, u32[]{:S(2)}, u32[]{:S(2)}) collective-permute-start(bf16[24,4096]{1,0:T(8,128)(2,1)S(1)} %get-tuple-element.73), channel_id=1, source_target_pairs={{0,32},{8,40},{16,48},{24,56},{32,64},{40,72},{48,80},{56,88},{64,... | collective-permute-start | bytes 589832 | tf_op jit(solution)/shard_map/ppermute | solution.py:22
  118.6 9.9 %collective-permute-start.22 = (bf16[24,4096]{1,0:T(8,128)(2,1)S(1)}, bf16[24,4096]{1,0:T(8,128)(2,1)S(1)}, u32[]{:S(2)}, u32[]{:S(2)}) collective-permute-start(bf16[24,4096]{1,0:T(8,128)(2,1)S(1)} %get-tuple-element.73), channel_id=1, source_target_pairs={{0,96},{8,104},{16,112},{24,120},{32,0},{40,8},{48,16},{56,24},{64... | collective-permute-start | bytes 589832 | tf_op jit(solution)/shard_map/ppermute | solution.py:22
  119.1 12.2 %collective-permute-start.18 = (bf16[24,4096]{1,0:T(8,128)(2,1)S(1)}, bf16[24,4096]{1,0:T(8,128)(2,1)S(1)}, u32[]{:S(2)}, u32[]{:S(2)}) collective-permute-start(bf16[24,4096]{1,0:T(8,128)(2,1)S(1)} %get-tuple-element.74), channel_id=1, source_target_pairs={{0,16},{8,24},{16,0},{24,8},{32,48},{40,56},{48,32},{56,40},{64,80... | collective-permute-start | bytes 589832 | tf_op jit(solution)/shard_map/ppermute | solution.py:22
  122.7 8.6 %collective-permute-start.17 = (bf16[24,4096]{1,0:T(8,128)(2,1)S(1)}, bf16[24,4096]{1,0:T(8,128)(2,1)S(1)}, u32[]{:S(2)}, u32[]{:S(2)}) collective-permute-start(bf16[24,4096]{1,0:T(8,128)(2,1)S(1)} %get-tuple-element.74), channel_id=1, source_target_pairs={{0,8},{8,16},{16,24},{24,0},{32,40},{40,48},{48,56},{56,32},{64,72... | collective-permute-start | bytes 589832 | tf_op jit(solution)/shard_map/ppermute | solution.py:22
  123.0 8.3 %collective-permute-start.19 = (bf16[24,4096]{1,0:T(8,128)(2,1)S(1)}, bf16[24,4096]{1,0:T(8,128)(2,1)S(1)}, u32[]{:S(2)}, u32[]{:S(2)}) collective-permute-start(bf16[24,4096]{1,0:T(8,128)(2,1)S(1)} %get-tuple-element.74), channel_id=1, source_target_pairs={{0,24},{8,0},{16,8},{24,16},{32,56},{40,32},{48,40},{56,48},{64,88... | collective-permute-start | bytes 589832 | tf_op jit(solution)/shard_map/ppermute | solution.py:22
  128.6 19.9 %collective-permute-start.25 = (bf16[4,24,4096]{2,1,0:T(8,128)(2,1)S(1)}, bf16[4,24,4096]{2,1,0:T(8,128)(2,1)S(1)}, u32[]{:S(2)}, u32[]{:S(2)}) collective-permute-start(bf16[4,24,4096]{2,1,0:T(8,128)(2,1)S(1)} %get-tuple-element.68), channel_id=1, source_target_pairs={{0,8},{8,16},{16,24},{24,0},{32,40},{40,48},{48,56},{56,32},{64,72... | collective-permute-start | bytes 2359304 | tf_op jit(solution)/shard_map/ppermute | solution.py:22
  129.7 19.7 %collective-permute-start.26 = (bf16[4,24,4096]{2,1,0:T(8,128)(2,1)S(1)}, bf16[4,24,4096]{2,1,0:T(8,128)(2,1)S(1)}, u32[]{:S(2)}, u32[]{:S(2)}) collective-permute-start(bf16[4,24,4096]{2,1,0:T(8,128)(2,1)S(1)} %get-tuple-element.68), channel_id=1, source_target_pairs={{0,24},{8,0},{16,8},{24,16},{32,56},{40,32},{48,40},{56,48},{64,88... | collective-permute-start | bytes 2359304 | tf_op jit(solution)/shard_map/ppermute | solution.py:22
  131.5 19.9 %collective-permute-start.23 = (bf16[4,24,4096]{2,1,0:T(8,128)(2,1)S(1)}, bf16[4,24,4096]{2,1,0:T(8,128)(2,1)S(1)}, u32[]{:S(2)}, u32[]{:S(2)}) collective-permute-start(bf16[4,24,4096]{2,1,0:T(8,128)(2,1)S(1)} %get-tuple-element.66), channel_id=1, source_target_pairs={{0,32},{8,40},{16,48},{24,56},{32,64},{40,72},{48,80},{56,88},{64,... | collective-permute-start | bytes 2359304 | tf_op jit(solution)/shard_map/ppermute | solution.py:22
  132.0 19.9 %collective-permute-start.24 = (bf16[4,24,4096]{2,1,0:T(8,128)(2,1)S(1)}, bf16[4,24,4096]{2,1,0:T(8,128)(2,1)S(1)}, u32[]{:S(2)}, u32[]{:S(2)}) collective-permute-start(bf16[4,24,4096]{2,1,0:T(8,128)(2,1)S(1)} %get-tuple-element.66), channel_id=1, source_target_pairs={{0,96},{8,104},{16,112},{24,120},{32,0},{40,8},{48,16},{56,24},{64... | collective-permute-start | bytes 2359304 | tf_op jit(solution)/shard_map/ppermute | solution.py:22
  148.5 14.2 %collective-permute-start.29 = (bf16[2,24,4096]{2,1,0:T(8,128)(2,1)S(1)}, bf16[2,24,4096]{2,1,0:T(8,128)(2,1)S(1)}, u32[]{:S(2)}, u32[]{:S(2)}) collective-permute-start(bf16[2,24,4096]{2,1,0:T(8,128)(2,1)S(1)} %slice.306), channel_id=1, source_target_pairs={{0,8},{8,16},{16,24},{24,0},{32,40},{40,48},{48,56},{56,32},{64,72... | collective-permute-start | bytes 1179656 | tf_op jit(solution)/shard_map/ppermute | solution.py:22
  149.5 13.3 %collective-permute-start.30 = (bf16[2,24,4096]{2,1,0:T(8,128)(2,1)S(1)}, bf16[2,24,4096]{2,1,0:T(8,128)(2,1)S(1)}, u32[]{:S(2)}, u32[]{:S(2)}) collective-permute-start(bf16[2,24,4096]{2,1,0:T(8,128)(2,1)S(1)} %slice.307), channel_id=1, source_target_pairs={{0,24},{8,0},{16,8},{24,16},{32,56},{40,32},{48,40},{56,48},{64,88... | collective-permute-start | bytes 1179656 | tf_op jit(solution)/shard_map/ppermute | solution.py:22
  151.4 11.5 %collective-permute-start.27 = (bf16[2,24,4096]{2,1,0:T(8,128)(2,1)S(1)}, bf16[2,24,4096]{2,1,0:T(8,128)(2,1)S(1)}, u32[]{:S(2)}, u32[]{:S(2)}) collective-permute-start(bf16[2,24,4096]{2,1,0:T(8,128)(2,1)S(1)} %slice.304), channel_id=1, source_target_pairs={{0,32},{8,40},{16,48},{24,56},{32,64},{40,72},{48,80},{56,88},{64,... | collective-permute-start | bytes 1179656 | tf_op jit(solution)/shard_map/ppermute | solution.py:22
  151.9 11.0 %collective-permute-start.28 = (bf16[2,24,4096]{2,1,0:T(8,128)(2,1)S(1)}, bf16[2,24,4096]{2,1,0:T(8,128)(2,1)S(1)}, u32[]{:S(2)}, u32[]{:S(2)}) collective-permute-start(bf16[2,24,4096]{2,1,0:T(8,128)(2,1)S(1)} %slice.305), channel_id=1, source_target_pairs={{0,96},{8,104},{16,112},{24,120},{32,0},{40,8},{48,16},{56,24},{64... | collective-permute-start | bytes 1179656 | tf_op jit(solution)/shard_map/ppermute | solution.py:22
  167.6 8.2 %collective-permute-start.40 = (bf16[2,24,4096]{2,1,0:T(8,128)(2,1)S(1)}, bf16[2,24,4096]{2,1,0:T(8,128)(2,1)S(1)}, u32[]{:S(2)}, u32[]{:S(2)}) collective-permute-start(bf16[2,24,4096]{2,1,0:T(8,128)(2,1)S(1)} %bitcast.254), channel_id=1, source_target_pairs={{0,24},{8,0},{16,8},{24,16},{32,56},{40,32},{48,40},{56,48},{64,88... | collective-permute-start | bytes 1179656 | tf_op jit(solution)/shard_map/ppermute | solution.py:22
  168.0 7.9 %collective-permute-start.31 = (bf16[2,24,4096]{2,1,0:T(8,128)(2,1)S(1)}, bf16[2,24,4096]{2,1,0:T(8,128)(2,1)S(1)}, u32[]{:S(2)}, u32[]{:S(2)}) collective-permute-start(bf16[2,24,4096]{2,1,0:T(8,128)(2,1)S(1)} %bitcast.253), channel_id=1, source_target_pairs={{0,32},{8,40},{16,48},{24,56},{32,64},{40,72},{48,80},{56,88},{64,... | collective-permute-start | bytes 1179656 | tf_op jit(solution)/shard_map/ppermute | solution.py:22
  168.0 7.9 %collective-permute-start.38 = (bf16[2,24,4096]{2,1,0:T(8,128)(2,1)S(1)}, bf16[2,24,4096]{2,1,0:T(8,128)(2,1)S(1)}, u32[]{:S(2)}, u32[]{:S(2)}) collective-permute-start(bf16[2,24,4096]{2,1,0:T(8,128)(2,1)S(1)} %bitcast.252), channel_id=1, source_target_pairs={{0,8},{8,16},{16,24},{24,0},{32,40},{40,48},{48,56},{56,32},{64,72... | collective-permute-start | bytes 1179656 | tf_op jit(solution)/shard_map/ppermute | solution.py:22
  169.1 7.8 %collective-permute-start.33 = (bf16[2,24,4096]{2,1,0:T(8,128)(2,1)S(1)}, bf16[2,24,4096]{2,1,0:T(8,128)(2,1)S(1)}, u32[]{:S(2)}, u32[]{:S(2)}) collective-permute-start(bf16[2,24,4096]{2,1,0:T(8,128)(2,1)S(1)} %bitcast.251), channel_id=1, source_target_pairs={{0,96},{8,104},{16,112},{24,120},{32,0},{40,8},{48,16},{56,24},{64... | collective-permute-start | bytes 1179656 | tf_op jit(solution)/shard_map/ppermute | solution.py:22
  177.5 16.1 %collective-permute-start.39 = (bf16[4,24,4096]{2,1,0:T(8,128)(2,1)S(1)}, bf16[4,24,4096]{2,1,0:T(8,128)(2,1)S(1)}, u32[]{:S(2)}, u32[]{:S(2)}) collective-permute-start(bf16[4,24,4096]{2,1,0:T(8,128)(2,1)S(1)} %pad_maximum_fusion.8), channel_id=1, source_target_pairs={{0,8},{8,16},{16,24},{24,0},{32,40},{40,48},{48,56},{56,32},{64,72... | collective-permute-start | bytes 2359304 | tf_op jit(solution)/shard_map/ppermute | solution.py:22
  179.0 15.4 %collective-permute-start.41 = (bf16[4,24,4096]{2,1,0:T(8,128)(2,1)S(1)}, bf16[4,24,4096]{2,1,0:T(8,128)(2,1)S(1)}, u32[]{:S(2)}, u32[]{:S(2)}) collective-permute-start(bf16[4,24,4096]{2,1,0:T(8,128)(2,1)S(1)} %pad_maximum_fusion.9), channel_id=1, source_target_pairs={{0,24},{8,0},{16,8},{24,16},{32,56},{40,32},{48,40},{56,48},{64,88... | collective-permute-start | bytes 2359304 | tf_op jit(solution)/shard_map/ppermute | solution.py:22
  180.7 17.4 %collective-permute-start.34 = (bf16[4,24,4096]{2,1,0:T(8,128)(2,1)S(1)}, bf16[4,24,4096]{2,1,0:T(8,128)(2,1)S(1)}, u32[]{:S(2)}, u32[]{:S(2)}) collective-permute-start(bf16[4,24,4096]{2,1,0:T(8,128)(2,1)S(1)} %pad_maximum_fusion.7), channel_id=1, source_target_pairs={{0,96},{8,104},{16,112},{24,120},{32,0},{40,8},{48,16},{56,24},{64... | collective-permute-start | bytes 2359304 | tf_op jit(solution)/shard_map/ppermute | solution.py:22
  184.3 15.3 %collective-permute-start.32 = (bf16[4,24,4096]{2,1,0:T(8,128)(2,1)S(1)}, bf16[4,24,4096]{2,1,0:T(8,128)(2,1)S(1)}, u32[]{:S(2)}, u32[]{:S(2)}) collective-permute-start(bf16[4,24,4096]{2,1,0:T(8,128)(2,1)S(1)} %pad_maximum_fusion.6), channel_id=1, source_target_pairs={{0,32},{8,40},{16,48},{24,56},{32,64},{40,72},{48,80},{56,88},{64,... | collective-permute-start | bytes 2359304 | tf_op jit(solution)/shard_map/ppermute | solution.py:22
  194.7 8.5 %collective-permute-start.42 = (bf16[24,4096]{1,0:T(8,128)(2,1)S(1)}, bf16[24,4096]{1,0:T(8,128)(2,1)S(1)}, u32[]{:S(2)}, u32[]{:S(2)}) collective-permute-start(bf16[24,4096]{1,0:T(8,128)(2,1)S(1)} %get-tuple-element.62), channel_id=1, source_target_pairs={{0,96},{8,104},{16,112},{24,120},{32,0},{40,8},{48,16},{56,24},{64... | collective-permute-start | bytes 589832 | tf_op jit(solution)/shard_map/ppermute | solution.py:22
  197.5 8.1 %collective-permute-start.44 = (bf16[24,4096]{1,0:T(8,128)(2,1)S(1)}, bf16[24,4096]{1,0:T(8,128)(2,1)S(1)}, u32[]{:S(2)}, u32[]{:S(2)}) collective-permute-start(bf16[24,4096]{1,0:T(8,128)(2,1)S(1)} %get-tuple-element.63), channel_id=1, source_target_pairs={{0,64},{8,72},{16,80},{24,88},{32,96},{40,104},{48,112},{56,120},{... | collective-permute-start | bytes 589832 | tf_op jit(solution)/shard_map/ppermute | solution.py:22
  197.5 10.4 %collective-permute-start.43 = (bf16[24,4096]{1,0:T(8,128)(2,1)S(1)}, bf16[24,4096]{1,0:T(8,128)(2,1)S(1)}, u32[]{:S(2)}, u32[]{:S(2)}) collective-permute-start(bf16[24,4096]{1,0:T(8,128)(2,1)S(1)} %get-tuple-element.64), channel_id=1, source_target_pairs={{0,32},{8,40},{16,48},{24,56},{32,64},{40,72},{48,80},{56,88},{64,... | collective-permute-start | bytes 589832 | tf_op jit(solution)/shard_map/ppermute | solution.py:22
  199.9 8.2 %collective-permute-start.35 = (bf16[24,4096]{1,0:T(8,128)(2,1)S(1)}, bf16[24,4096]{1,0:T(8,128)(2,1)S(1)}, u32[]{:S(2)}, u32[]{:S(2)}) collective-permute-start(bf16[24,4096]{1,0:T(8,128)(2,1)S(1)} %get-tuple-element.59), channel_id=1, source_target_pairs={{0,24},{8,0},{16,8},{24,16},{32,56},{40,32},{48,40},{56,48},{64,88... | collective-permute-start | bytes 589832 | tf_op jit(solution)/shard_map/ppermute | solution.py:22
  201.3 6.8 %collective-permute-start.37 = (bf16[24,4096]{1,0:T(8,128)(2,1)S(1)}, bf16[24,4096]{1,0:T(8,128)(2,1)S(1)}, u32[]{:S(2)}, u32[]{:S(2)}) collective-permute-start(bf16[24,4096]{1,0:T(8,128)(2,1)S(1)} %get-tuple-element.60), channel_id=1, source_target_pairs={{0,16},{8,24},{16,0},{24,8},{32,48},{40,56},{48,32},{56,40},{64,80... | collective-permute-start | bytes 589832 | tf_op jit(solution)/shard_map/ppermute | solution.py:22
  203.2 6.5 %collective-permute-start.36 = (bf16[24,4096]{1,0:T(8,128)(2,1)S(1)}, bf16[24,4096]{1,0:T(8,128)(2,1)S(1)}, u32[]{:S(2)}, u32[]{:S(2)}) collective-permute-start(bf16[24,4096]{1,0:T(8,128)(2,1)S(1)} %get-tuple-element.61), channel_id=1, source_target_pairs={{0,8},{8,16},{16,24},{24,0},{32,40},{40,48},{48,56},{56,32},{64,72... | collective-permute-start | bytes 589832 | tf_op jit(solution)/shard_map/ppermute | solution.py:22
  210.8 23.3 %all-to-all-start.2 = ((bf16[8,48,512]{2,1,0:T(8,128)(2,1)}), bf16[8,48,512]{2,1,0:T(8,128)(2,1)S(1)}, u32[]{:S(2)}, u32[]{:S(2)}) async-start(bf16[8,48,512]{2,1,0:T(8,128)(2,1)} %copy.55), calls=%async_computation.2 | async-start | bytes 786432 | tf_op jit(solution)/shard_map/all_to_all | solution.py:359
  (20 other events, 182.1 us)
